TPU v7x, 32 devices: a whole 2x2x4 slice. The times are simulated.
32 devices in a mesh: rep: 4 (over x, core), shard: 8 (over z, y).
Axes of the slice: x: 2, y: 2, z: 4, core: 2. Of those that a mesh axis runs over, the one named last changes fastest.
Arguments:
- block_input: float32 [32, 256, 768], P(('rep', 'shard')), may hold values from -6 to 6
- attn_gain: bfloat16 [768], P('shard'), may hold values from 0.099609375 to 1.8984375
- attn_shift: bfloat16 [768], P('shard'), may hold values from -3 to 3
- query_weight: bfloat16 [768, 768], P('shard'), may hold values from -4 to 4
- query_bias: bfloat16 [768], P('shard'), may hold values from -3 to 3
- key_weight: bfloat16 [768, 768], P('shard'), may hold values from -4 to 4
- value_weight: bfloat16 [768, 768], P('shard'), may hold values from -0.21875 to 0.21875
- value_bias: bfloat16 [768], P('shard'), may hold values from -0.3125 to 0.3125
- out_weight: bfloat16 [768, 768], P('shard'), may hold values from -3.5 to 3.5
- out_bias: bfloat16 [768], P('shard'), may hold values from -3 to 3
- mlp_gain: bfloat16 [768], P('shard'), may hold values from 0.099609375 to 1.8984375
- mlp_shift: bfloat16 [768], P('shard'), may hold values from -3 to 3
- hidden_weight: bfloat16 [768, 3072], P('shard'), may hold values from -0.21875 to 0.21875
- hidden_bias: bfloat16 [3072], P('shard'), may hold values from -3 to 3
- proj_weight: bfloat16 [3072, 768], P('shard'), may hold values from -0.109375 to 0.109375
- proj_bias: bfloat16 [768], P('shard'), may hold values from -3 to 3
- out_cotangent: float32 [32, 256, 768], P(('rep', 'shard')), may hold values from -6 to 6
Outputs:
- block_output: float32 [32, 256, 768], P(('rep', 'shard'))
- input_grad: float32 [32, 256, 768], P(('rep', 'shard'))
- attn_gain_grad: float32 [768], P('shard')
- attn_shift_grad: float32 [768], P('shard')
- query_weight_grad: float32 [768, 768], P('shard')
- query_bias_grad: float32 [768], P('shard')
- key_weight_grad: float32 [768, 768], P('shard')
- value_weight_grad: float32 [768, 768], P('shard')
- value_bias_grad: float32 [768], P('shard')
- out_weight_grad: float32 [768, 768], P('shard')
- out_bias_grad: float32 [768], P('shard')
- mlp_gain_grad: float32 [768], P('shard')
- mlp_shift_grad: float32 [768], P('shard')
- hidden_weight_grad: float32 [768, 3072], P('shard')
- hidden_bias_grad: float32 [3072], P('shard')
- proj_weight_grad: float32 [3072, 768], P('shard')
- proj_bias_grad: float32 [768], P('shard')
All inputs are finite; a program needn't handle non-finite values.
Results may differ from a plain program's by a relative error of at most 0.02.
The roundings to bfloat16 on the way count: a program that leaves them out, or rounds other values in their place, can miss the bound.
Values may be sent and summed in bfloat16 or wider, within the bound.
A program may use at most 128 MiB of HBM per device.

v0:
```python
import jax
import jax.numpy as jnp
from jax import lax
from jax.sharding import PartitionSpec as P

HD = 64


EPS = 1e-05
ROOT_HALF = 0.7071067811865476
INV_ROOT_TWO_PI = 0.3989422804014327


def layer_norm(tokens, norm_gain, norm_shift):
    average = jnp.mean(tokens, axis=-1, keepdims=True)
    centered = tokens - average
    inv_std = lax.rsqrt(jnp.mean(centered * centered, axis=-1, keepdims=True) + EPS)
    normed = centered * inv_std
    shaped = normed * norm_gain.astype(jnp.float32) + norm_shift.astype(jnp.float32)
    return (normed, inv_std, shaped.astype(jnp.bfloat16))


def norm_grad(upstream, normed, inv_std, norm_gain):
    scaled = upstream * norm_gain.astype(jnp.float32)
    inner = (
        scaled
        - jnp.mean(scaled, axis=-1, keepdims=True)
        - normed * jnp.mean(scaled * normed, axis=-1, keepdims=True)
    )
    return (inner * inv_std, jnp.sum(upstream * normed, axis=0), jnp.sum(upstream, axis=0))


def matmul(left, right):
    return jnp.dot(left, right, preferred_element_type=jnp.float32)


def times_transposed(left, right):
    return lax.dot_general(
        left, right, (((1,), (1,)), ((), ())), preferred_element_type=jnp.float32
    )


def token_sum(left, right):
    return lax.dot_general(
        left, right, (((0,), (0,)), ((), ())), preferred_element_type=jnp.float32
    )


def gelu_parts(before):
    normal_cdf = 0.5 * (1.0 + lax.erf(before * ROOT_HALF))
    return (
        before * normal_cdf,
        normal_cdf + before * INV_ROOT_TWO_PI * jnp.exp(-0.5 * before * before),
    )


def attend(query, keys, values):
    factor = query.shape[-1] ** (-0.5)
    scores = jnp.einsum("clhd,cmhd->chlm", query, keys, preferred_element_type=jnp.float32) * factor
    row_top = jnp.max(scores, axis=-1, keepdims=True)
    log_total = row_top + jnp.log(jnp.sum(jnp.exp(scores - row_top), axis=-1, keepdims=True))
    weights = jnp.exp(scores - log_total).astype(jnp.bfloat16)
    mixed = jnp.einsum(
        "chlm,cmhd->clhd", weights, values, preferred_element_type=jnp.float32
    ).astype(jnp.bfloat16)
    return (mixed, log_total)


def attend_grad(query, keys, values, mixed, log_total, grad_mixed):
    factor = query.shape[-1] ** (-0.5)
    scores = jnp.einsum("clhd,cmhd->chlm", query, keys, preferred_element_type=jnp.float32) * factor
    weights = jnp.exp(scores - log_total)
    weights_low = weights.astype(jnp.bfloat16)
    grad_values = jnp.einsum(
        "chlm,clhd->cmhd", weights_low, grad_mixed, preferred_element_type=jnp.float32
    )
    grad_weights = jnp.einsum(
        "clhd,cmhd->chlm", grad_mixed, values, preferred_element_type=jnp.float32
    )
    delta = jnp.sum(grad_mixed.astype(jnp.float32) * mixed.astype(jnp.float32), axis=-1)
    delta = jnp.transpose(delta, (0, 2, 1))[..., None]
    grad_scores = (weights * (grad_weights - delta)).astype(jnp.bfloat16)
    grad_query = (
        jnp.einsum("chlm,cmhd->clhd", grad_scores, keys, preferred_element_type=jnp.float32)
        * factor
    )
    grad_keys = (
        jnp.einsum("chlm,clhd->cmhd", grad_scores, query, preferred_element_type=jnp.float32)
        * factor
    )
    return (grad_query, grad_keys, grad_values)


def on_device(
    block_input,
    attn_gain,
    attn_shift,
    query_weight,
    query_bias,
    key_weight,
    value_weight,
    value_bias,
    out_weight,
    out_bias,
    mlp_gain,
    mlp_shift,
    hidden_weight,
    hidden_bias,
    proj_weight,
    proj_bias,
    out_cotangent,
):
    clip_count, frame_count, model_width = block_input.shape
    head_count = model_width // HD
    token_count = clip_count * frame_count

    def split_heads(matrix):
        return matrix.reshape(clip_count, frame_count, head_count, HD)

    def join_heads(tensor):
        return tensor.reshape(token_count, model_width)

    residual = block_input.reshape(token_count, model_width)
    (
        attn_gain_all,
        attn_shift_all,
        query_all,
        query_bias_all,
        key_all,
        value_all,
        value_bias_all,
        out_all,
        out_bias_all,
    ) = (
        lax.all_gather(attn_gain, "shard", axis=0, tiled=True),
        lax.all_gather(attn_shift, "shard", axis=0, tiled=True),
        lax.all_gather(query_weight, "shard", axis=0, tiled=True),
        lax.all_gather(query_bias, "shard", axis=0, tiled=True),
        lax.all_gather(key_weight, "shard", axis=0, tiled=True),
        lax.all_gather(value_weight, "shard", axis=0, tiled=True),
        lax.all_gather(value_bias, "shard", axis=0, tiled=True),
        lax.all_gather(out_weight, "shard", axis=0, tiled=True),
        lax.all_gather(out_bias, "shard", axis=0, tiled=True),
    )
    normed_one, inv_one, input_low = layer_norm(residual, attn_gain_all, attn_shift_all)
    query_low = (matmul(input_low, query_all) + query_bias_all.astype(jnp.float32)).astype(
        jnp.bfloat16
    )
    keys_low = matmul(input_low, key_all).astype(jnp.bfloat16)
    values_low = (matmul(input_low, value_all) + value_bias_all.astype(jnp.float32)).astype(
        jnp.bfloat16
    )
    mixed, log_total = attend(
        split_heads(query_low), split_heads(keys_low), split_heads(values_low)
    )
    mixed_rows = join_heads(mixed)
    middle = residual + matmul(mixed_rows, out_all) + out_bias_all.astype(jnp.float32)
    mlp_gain_all, mlp_shift_all, hidden_all, hidden_bias_all, proj_all, proj_bias_all = (
        lax.all_gather(mlp_gain, "shard", axis=0, tiled=True),
        lax.all_gather(mlp_shift, "shard", axis=0, tiled=True),
        lax.all_gather(hidden_weight, "shard", axis=0, tiled=True),
        lax.all_gather(hidden_bias, "shard", axis=0, tiled=True),
        lax.all_gather(proj_weight, "shard", axis=0, tiled=True),
        lax.all_gather(proj_bias, "shard", axis=0, tiled=True),
    )
    normed_two, inv_two, middle_low = layer_norm(middle, mlp_gain_all, mlp_shift_all)
    before_act = matmul(middle_low, hidden_all) + hidden_bias_all.astype(jnp.float32)
    activated, slope = gelu_parts(before_act)
    act_low = activated.astype(jnp.bfloat16)
    block_output = middle + matmul(act_low, proj_all) + proj_bias_all.astype(jnp.float32)
    mlp_gain_all, mlp_shift_all, hidden_all, hidden_bias_all, proj_all, proj_bias_all = (
        lax.all_gather(mlp_gain, "shard", axis=0, tiled=True),
        lax.all_gather(mlp_shift, "shard", axis=0, tiled=True),
        lax.all_gather(hidden_weight, "shard", axis=0, tiled=True),
        lax.all_gather(hidden_bias, "shard", axis=0, tiled=True),
        lax.all_gather(proj_weight, "shard", axis=0, tiled=True),
        lax.all_gather(proj_bias, "shard", axis=0, tiled=True),
    )
    upstream = out_cotangent.reshape(token_count, model_width)
    up_low = upstream.astype(jnp.bfloat16)
    proj_term = token_sum(act_low, up_low)
    proj_bias_term = jnp.sum(upstream, axis=0)
    grad_before = times_transposed(up_low, proj_all) * slope
    before_low = grad_before.astype(jnp.bfloat16)
    hidden_term = token_sum(middle_low, before_low)
    hidden_bias_term = jnp.sum(grad_before, axis=0)
    grad_normed_two = times_transposed(before_low, hidden_all)
    grad_middle_norm, mlp_gain_term, mlp_shift_term = norm_grad(
        grad_normed_two, normed_two, inv_two, mlp_gain_all
    )
    grad_middle = upstream + grad_middle_norm
    mlp_owned = (
        lax.psum_scatter(mlp_gain_term, "shard", scatter_dimension=0, tiled=True),
        lax.psum_scatter(mlp_shift_term, "shard", scatter_dimension=0, tiled=True),
        lax.psum_scatter(hidden_term, "shard", scatter_dimension=0, tiled=True),
        lax.psum_scatter(hidden_bias_term, "shard", scatter_dimension=0, tiled=True),
        lax.psum_scatter(proj_term, "shard", scatter_dimension=0, tiled=True),
        lax.psum_scatter(proj_bias_term, "shard", scatter_dimension=0, tiled=True),
    )
    (
        mlp_gain_share,
        mlp_shift_share,
        hidden_weight_share,
        hidden_bias_share,
        proj_weight_share,
        proj_bias_share,
    ) = (
        lax.psum_scatter(
            mlp_owned[0].astype(jnp.bfloat16), "rep", scatter_dimension=0, tiled=True
        ).astype(jnp.float32),
        lax.psum_scatter(
            mlp_owned[1].astype(jnp.bfloat16), "rep", scatter_dimension=0, tiled=True
        ).astype(jnp.float32),
        lax.psum_scatter(
            mlp_owned[2].astype(jnp.bfloat16), "rep", scatter_dimension=0, tiled=True
        ).astype(jnp.float32),
        lax.psum_scatter(
            mlp_owned[3].astype(jnp.bfloat16), "rep", scatter_dimension=0, tiled=True
        ).astype(jnp.float32),
        lax.psum_scatter(
            mlp_owned[4].astype(jnp.bfloat16), "rep", scatter_dimension=0, tiled=True
        ).astype(jnp.float32),
        lax.psum_scatter(
            mlp_owned[5].astype(jnp.bfloat16), "rep", scatter_dimension=0, tiled=True
        ).astype(jnp.float32),
    )
    (
        attn_gain_all,
        attn_shift_all,
        query_all,
        query_bias_all,
        key_all,
        value_all,
        value_bias_all,
        out_all,
        out_bias_all,
    ) = (
        lax.all_gather(attn_gain, "shard", axis=0, tiled=True),
        lax.all_gather(attn_shift, "shard", axis=0, tiled=True),
        lax.all_gather(query_weight, "shard", axis=0, tiled=True),
        lax.all_gather(query_bias, "shard", axis=0, tiled=True),
        lax.all_gather(key_weight, "shard", axis=0, tiled=True),
        lax.all_gather(value_weight, "shard", axis=0, tiled=True),
        lax.all_gather(value_bias, "shard", axis=0, tiled=True),
        lax.all_gather(out_weight, "shard", axis=0, tiled=True),
        lax.all_gather(out_bias, "shard", axis=0, tiled=True),
    )
    middle_grad_low = grad_middle.astype(jnp.bfloat16)
    out_term = token_sum(mixed_rows, middle_grad_low)
    out_bias_term = jnp.sum(grad_middle, axis=0)
    grad_mixed = times_transposed(middle_grad_low, out_all).astype(jnp.bfloat16)
    grad_query, grad_keys, grad_values = attend_grad(
        split_heads(query_low),
        split_heads(keys_low),
        split_heads(values_low),
        mixed,
        log_total,
        split_heads(grad_mixed),
    )
    grad_query = join_heads(grad_query)
    grad_keys = join_heads(grad_keys)
    grad_values = join_heads(grad_values)
    query_bias_term = jnp.sum(grad_query, axis=0)
    value_bias_term = jnp.sum(grad_values, axis=0)
    query_grad_low = grad_query.astype(jnp.bfloat16)
    key_grad_low = grad_keys.astype(jnp.bfloat16)
    value_grad_low = grad_values.astype(jnp.bfloat16)
    query_term = token_sum(input_low, query_grad_low)
    key_term = token_sum(input_low, key_grad_low)
    value_term = token_sum(input_low, value_grad_low)
    grad_normed_one = (
        times_transposed(query_grad_low, query_all)
        + times_transposed(key_grad_low, key_all)
        + times_transposed(value_grad_low, value_all)
    )
    grad_input_norm, attn_gain_term, attn_shift_term = norm_grad(
        grad_normed_one, normed_one, inv_one, attn_gain_all
    )
    input_grad = grad_middle + grad_input_norm
    attn_owned = (
        lax.psum_scatter(attn_gain_term, "shard", scatter_dimension=0, tiled=True),
        lax.psum_scatter(attn_shift_term, "shard", scatter_dimension=0, tiled=True),
        lax.psum_scatter(query_term, "shard", scatter_dimension=0, tiled=True),
        lax.psum_scatter(query_bias_term, "shard", scatter_dimension=0, tiled=True),
        lax.psum_scatter(key_term, "shard", scatter_dimension=0, tiled=True),
        lax.psum_scatter(value_term, "shard", scatter_dimension=0, tiled=True),
        lax.psum_scatter(value_bias_term, "shard", scatter_dimension=0, tiled=True),
        lax.psum_scatter(out_term, "shard", scatter_dimension=0, tiled=True),
        lax.psum_scatter(out_bias_term, "shard", scatter_dimension=0, tiled=True),
    )
    (
        attn_gain_share,
        attn_shift_share,
        query_weight_share,
        query_bias_share,
        key_weight_share,
        value_weight_share,
        value_bias_share,
        out_weight_share,
        out_bias_share,
    ) = (
        lax.psum_scatter(
            attn_owned[0].astype(jnp.bfloat16), "rep", scatter_dimension=0, tiled=True
        ).astype(jnp.float32),
        lax.psum_scatter(
            attn_owned[1].astype(jnp.bfloat16), "rep", scatter_dimension=0, tiled=True
        ).astype(jnp.float32),
        lax.psum_scatter(
            attn_owned[2].astype(jnp.bfloat16), "rep", scatter_dimension=0, tiled=True
        ).astype(jnp.float32),
        lax.psum_scatter(
            attn_owned[3].astype(jnp.bfloat16), "rep", scatter_dimension=0, tiled=True
        ).astype(jnp.float32),
        lax.psum_scatter(
            attn_owned[4].astype(jnp.bfloat16), "rep", scatter_dimension=0, tiled=True
        ).astype(jnp.float32),
        lax.psum_scatter(
            attn_owned[5].astype(jnp.bfloat16), "rep", scatter_dimension=0, tiled=True
        ).astype(jnp.float32),
        lax.psum_scatter(
            attn_owned[6].astype(jnp.bfloat16), "rep", scatter_dimension=0, tiled=True
        ).astype(jnp.float32),
        lax.psum_scatter(
            attn_owned[7].astype(jnp.bfloat16), "rep", scatter_dimension=0, tiled=True
        ).astype(jnp.float32),
        lax.psum_scatter(
            attn_owned[8].astype(jnp.bfloat16), "rep", scatter_dimension=0, tiled=True
        ).astype(jnp.float32),
    )
    (
        attn_gain_grad,
        attn_shift_grad,
        query_weight_grad,
        query_bias_grad,
        key_weight_grad,
        value_weight_grad,
        value_bias_grad,
        out_weight_grad,
        out_bias_grad,
        mlp_gain_grad,
        mlp_shift_grad,
        hidden_weight_grad,
        hidden_bias_grad,
        proj_weight_grad,
        proj_bias_grad,
    ) = (
        lax.all_gather(attn_gain_share.astype(jnp.bfloat16), "rep", axis=0, tiled=True).astype(
            attn_gain_share.dtype
        ),
        lax.all_gather(attn_shift_share.astype(jnp.bfloat16), "rep", axis=0, tiled=True).astype(
            attn_shift_share.dtype
        ),
        lax.all_gather(query_weight_share.astype(jnp.bfloat16), "rep", axis=0, tiled=True).astype(
            query_weight_share.dtype
        ),
        lax.all_gather(query_bias_share.astype(jnp.bfloat16), "rep", axis=0, tiled=True).astype(
            query_bias_share.dtype
        ),
        lax.all_gather(key_weight_share.astype(jnp.bfloat16), "rep", axis=0, tiled=True).astype(
            key_weight_share.dtype
        ),
        lax.all_gather(value_weight_share.astype(jnp.bfloat16), "rep", axis=0, tiled=True).astype(
            value_weight_share.dtype
        ),
        lax.all_gather(value_bias_share.astype(jnp.bfloat16), "rep", axis=0, tiled=True).astype(
            value_bias_share.dtype
        ),
        lax.all_gather(out_weight_share.astype(jnp.bfloat16), "rep", axis=0, tiled=True).astype(
            out_weight_share.dtype
        ),
        lax.all_gather(out_bias_share.astype(jnp.bfloat16), "rep", axis=0, tiled=True).astype(
            out_bias_share.dtype
        ),
        lax.all_gather(mlp_gain_share.astype(jnp.bfloat16), "rep", axis=0, tiled=True).astype(
            mlp_gain_share.dtype
        ),
        lax.all_gather(mlp_shift_share.astype(jnp.bfloat16), "rep", axis=0, tiled=True).astype(
            mlp_shift_share.dtype
        ),
        lax.all_gather(hidden_weight_share.astype(jnp.bfloat16), "rep", axis=0, tiled=True).astype(
            hidden_weight_share.dtype
        ),
        lax.all_gather(hidden_bias_share.astype(jnp.bfloat16), "rep", axis=0, tiled=True).astype(
            hidden_bias_share.dtype
        ),
        lax.all_gather(proj_weight_share.astype(jnp.bfloat16), "rep", axis=0, tiled=True).astype(
            proj_weight_share.dtype
        ),
        lax.all_gather(proj_bias_share.astype(jnp.bfloat16), "rep", axis=0, tiled=True).astype(
            proj_bias_share.dtype
        ),
    )
    return (
        block_output.reshape(clip_count, frame_count, model_width),
        input_grad.reshape(clip_count, frame_count, model_width),
        attn_gain_grad,
        attn_shift_grad,
        query_weight_grad,
        query_bias_grad,
        key_weight_grad,
        value_weight_grad,
        value_bias_grad,
        out_weight_grad,
        out_bias_grad,
        mlp_gain_grad,
        mlp_shift_grad,
        hidden_weight_grad,
        hidden_bias_grad,
        proj_weight_grad,
        proj_bias_grad,
    )


def solution(mesh):
    placed = (
        P(("rep", "shard"), None, None),
        P("shard"),
        P("shard"),
        P("shard", None),
        P("shard"),
        P("shard", None),
        P("shard", None),
        P("shard"),
        P("shard", None),
        P("shard"),
        P("shard"),
        P("shard"),
        P("shard", None),
        P("shard"),
        P("shard", None),
        P("shard"),
        P(("rep", "shard"), None, None),
    )
    return jax.shard_map(
        on_device,
        mesh=mesh,
        in_specs=placed,
        out_specs=(
            P(("rep", "shard"), None, None),
            P(("rep", "shard"), None, None),
            P("shard"),
            P("shard"),
            P("shard", None),
            P("shard"),
            P("shard", None),
            P("shard", None),
            P("shard"),
            P("shard", None),
            P("shard"),
            P("shard"),
            P("shard"),
            P("shard", None),
            P("shard"),
            P("shard", None),
            P("shard"),
        ),
        check_vma=False,
    )
```

profile of v0, /device:TPU:0, one launch (start us, length us, event | category | flops | bytes accessed | tf_op | source)
XLA Modules:
  0.0 1122.5 jit_solution(13147129668082626300)
XLA Ops:
  20.6 39.6 %all-reduce.36 = (bf16[768]{0:T(1024)(128)(2,1)S(1)}, bf16[768]{0:T(1024)(128)(2,1)S(1)}, bf16[768]{0:T(1024)(128)(2,1)S(1)}, bf16[768]{0:T(1024)(128)(2,1)S(1)}...) all-reduce(bf16[768]{0:T(1024)(128)(2,1)S(1)} %dynamic-update-slice, ...), channel_id=1, replica_groups=mesh['rep'=4,'shard'=8] {'shard'}, use_global_device_ids=true, to_apply=%add.1 | all-reduce | flops 6144 | bytes 24576
  62.0 26.5 %all-gather = bf16[8,1,384]{2,1,0:T(2,128)(2,1)S(1)} all-gather(bf16[1,1,384]{2,1,0:T(2,128)(2,1)S(1)} %reshape.344), channel_id=1, replica_groups=mesh['rep'=4,'shard'=8] {'shard'}, dimensions={0}, use_global_device_ids=true | all-gather | bytes 6912 | tf_op jit(solution)/shard_map/all_gather | solution.py:162
  98.3 40.1 %all-gather.8.cloned.1.call-done = bf16[768,768]{1,0:T(8,128)(2,1)} async-done(((bf16[96,768]{1,0:T(8,128)(2,1)}), bf16[768,768]{1,0:T(8,128)(2,1)}) %all-gather.8.cloned.1.call-update) | async-done | bytes 1179664 | tf_op jit(solution)/shard_map/all_gather | solution.py:140
  144.0 36.3 %all-gather.14.cloned.1.call-done = bf16[768,768]{1,0:T(8,128)(2,1)} async-done(((bf16[96,768]{1,0:T(8,128)(2,1)}), bf16[768,768]{1,0:T(8,128)(2,1)}) %all-gather.14.cloned.1.call-update) | async-done | bytes 1179664 | tf_op jit(solution)/shard_map/all_gather | solution.py:142
  180.3 2.1 fusion.32
  184.0 76.3 %all-gather.16.cloned.1.call-done = bf16[768,3072]{1,0:T(8,128)(2,1)} async-done(((bf16[96,3072]{1,0:T(8,128)(2,1)}), bf16[768,3072]{1,0:T(8,128)(2,1)}) %all-gather.16.cloned.1.call-update) | async-done | bytes 4718608 | tf_op jit(solution)/shard_map/all_gather | solution.py:161
  260.3 6.5 multiply_convert_fusion.1
  266.9 73.2 %all-gather.18.cloned.1.call-done = bf16[3072,768]{1,0:T(8,128)(2,1)} async-done(((bf16[384,768]{1,0:T(8,128)(2,1)}), bf16[3072,768]{1,0:T(8,128)(2,1)}) %all-gather.18.cloned.1.call-update) | async-done | bytes 4718608 | tf_op jit(solution)/shard_map/all_gather | solution.py:163
  340.1 6.1 fusion.33
  346.3 2.2 multiply_reduce_fusion.1
  350.3 1.9 fusion.20
  352.3 2.8 convolution_convert_fusion
  355.1 1.9 copy.62
  357.0 2.5 fusion.28
  360.3 2.1 fusion.37
  362.7 2.0 copy.63
  366.1 2.1 multiply_convert_fusion
  369.6 2.2 fusion.39
  371.8 2.6 fusion.29
  374.5 2.1 fusion.41
  376.7 6.7 fusion.11
  384.5 6.5 fusion.34
  391.1 29.2 %reduce-scatter.25.cloned.1.call-done = f32[96,768]{1,0:T(8,128)} async-done(((f32[768,768]{1,0:T(8,128)}), f32[96,768]{1,0:T(8,128)}) %reduce-scatter.25.cloned.1.call-update) | async-done | bytes 294928 | tf_op jit(solution)/shard_map/reduce_scatter | solution.py:288
  422.0 70.7 %reduce-scatter.21.cloned.1.call-done = f32[96,768]{1,0:T(8,128)} async-done(((f32[768,768]{1,0:T(8,128)}), f32[96,768]{1,0:T(8,128)}) %reduce-scatter.21.cloned.1.call-update) | async-done | bytes 294928 | tf_op jit(solution)/shard_map/reduce_scatter | solution.py:286
  494.4 70.6 %reduce-scatter.17.cloned.1.call-done = f32[96,768]{1,0:T(8,128)} async-done(((f32[768,768]{1,0:T(8,128)}), f32[96,768]{1,0:T(8,128)}) %reduce-scatter.17.cloned.1.call-update) | async-done | bytes 294928 | tf_op jit(solution)/shard_map/reduce_scatter | solution.py:285
  566.8 70.5 %reduce-scatter.13.cloned.1.call-done = f32[96,768]{1,0:T(8,128)} async-done(((f32[768,768]{1,0:T(8,128)}), f32[96,768]{1,0:T(8,128)}) %reduce-scatter.13.cloned.1.call-update) | async-done | bytes 294928 | tf_op jit(solution)/shard_map/reduce_scatter | solution.py:283
  644.2 158.1 %reduce-scatter.29.cloned.1.call-done = f32[96,3072]{1,0:T(8,128)} async-done(((f32[768,3072]{1,0:T(8,128)}), f32[96,3072]{1,0:T(8,128)}) %reduce-scatter.29.cloned.1.call-update) | async-done | bytes 1179664 | tf_op jit(solution)/shard_map/reduce_scatter | solution.py:195
  802.3 2.2 convert_element_type.309
  804.5 2.8 fusion.45
  811.9 1.9 multiply_reduce_fusion.2
  813.9 38.5 %all-reduce.35 = (bf16[768]{0:T(1024)(128)(2,1)S(1)}, bf16[768]{0:T(1024)(128)(2,1)S(1)}, bf16[768]{0:T(1024)(128)(2,1)S(1)}, bf16[768]{0:T(1024)(128)(2,1)S(1)}...) all-reduce(f32[768]{0:T(1024)S(1)} %get-tuple-element.19, ...), channel_id=2, replica_groups=mesh['rep'=4,'shard'=8] {'shard'}, use_global_device_ids=true, to_apply=%region_12.0.clone | all-reduce | flops 9216 | bytes 55296
  853.1 6.1 all-reduce.38
  861.9 6.8 all-reduce.37
  873.4 95.0 %reduce-scatter.33.cloned.1.call-done = f32[384,768]{1,0:T(8,128)} async-done(((f32[3072,768]{1,0:T(8,128)}), f32[384,768]{1,0:T(8,128)}) %reduce-scatter.33.cloned.1.call-update) | async-done | bytes 1179664 | tf_op jit(solution)/shard_map/reduce_scatter | solution.py:197
  968.4 2.2 convert_element_type.313
  972.2 4.6 fusion.7
  976.9 13.3 %reduce-scatter.27.cloned.1.call-done = bf16[24,768]{1,0:T(8,128)(2,1)} async-done(((bf16[96,768]{1,0:T(8,128)(2,1)}), bf16[24,768]{1,0:T(8,128)(2,1)}) %reduce-scatter.27.cloned.1.call-update) | async-done | bytes 36880 | tf_op jit(solution)/shard_map/reduce_scatter | solution.py:323
  990.2 5.7 all_gather.120
  996.6 16.2 %reduce-scatter.23.cloned.1.call-done = bf16[24,768]{1,0:T(8,128)(2,1)} async-done(((bf16[96,768]{1,0:T(8,128)(2,1)}), bf16[24,768]{1,0:T(8,128)(2,1)}) %reduce-scatter.23.cloned.1.call-update) | async-done | bytes 36880 | tf_op jit(solution)/shard_map/reduce_scatter | solution.py:317
  1012.8 5.7 all_gather.118
  1019.2 16.2 %reduce-scatter.19.cloned.1.call-done = bf16[24,768]{1,0:T(8,128)(2,1)} async-done(((bf16[96,768]{1,0:T(8,128)(2,1)}), bf16[24,768]{1,0:T(8,128)(2,1)}) %reduce-scatter.19.cloned.1.call-update) | async-done | bytes 36880 | tf_op jit(solution)/shard_map/reduce_scatter | solution.py:314
  1035.4 5.7 all_gather.117
  1041.8 16.2 %reduce-scatter.15.cloned.1.call-done = bf16[24,768]{1,0:T(8,128)(2,1)} async-done(((bf16[96,768]{1,0:T(8,128)(2,1)}), bf16[24,768]{1,0:T(8,128)(2,1)}) %reduce-scatter.15.cloned.1.call-update) | async-done | bytes 36880 | tf_op jit(solution)/shard_map/reduce_scatter | solution.py:308
  1057.9 5.7 all_gather.115
  1064.3 18.6 %reduce-scatter.31.cloned.1.call-done = bf16[24,3072]{1,0:T(8,128)(2,1)} async-done(((bf16[96,3072]{1,0:T(8,128)(2,1)}), bf16[24,3072]{1,0:T(8,128)(2,1)}) %reduce-scatter.31.cloned.1.call-update) | async-done | bytes 147472 | tf_op jit(solution)/shard_map/reduce_scatter | solution.py:214
  1083.0 7.1 all_gather.124
  1091.2 16.2 %reduce-scatter.35.cloned.1.call-done = bf16[96,768]{1,0:T(8,128)(2,1)} async-done(((bf16[384,768]{1,0:T(8,128)(2,1)}), bf16[96,768]{1,0:T(8,128)(2,1)}) %reduce-scatter.35.cloned.1.call-update) | async-done | bytes 147472 | tf_op jit(solution)/shard_map/reduce_scatter | solution.py:220
  1107.4 7.2 all_gather.126
  (264 shorter events, 65.6 us)
Async XLA Ops:
  7.2 83.3 %copy-start = (f32[1,256,768]{2,1,0:T(8,128)S(1)}, f32[1,256,768]{2,1,0:T(8,128)}, u32[]{:S(2)}) copy-start(f32[1,256,768]{2,1,0:T(8,128)} %param.17) | copy-start | bytes 2359300
  7.2 84.6 %all-gather.10.cloned.1.call-start = ((), (), s32[]{:S(2)}) async-start(), calls=%async_computation.13 | async-start | bytes 1327104 | tf_op jit(solution)/shard_map/all_gather | solution.py:137
  7.9 88.4 %all-gather.12.cloned.1.call-start = ((), (), s32[]{:S(2)}) async-start(), calls=%async_computation.14 | async-start | bytes 1327104 | tf_op jit(solution)/shard_map/all_gather | solution.py:139
  8.7 129.7 %all-gather.8.cloned.1.call-start = ((), (), s32[]{:S(2)}) async-start(), calls=%async_computation.12 | async-start | bytes 1327104 | tf_op jit(solution)/shard_map/all_gather | solution.py:140
  9.4 170.8 %all-gather.14.cloned.1.call-start = ((), (), s32[]{:S(2)}) async-start(), calls=%async_computation.15 | async-start | bytes 1327104 | tf_op jit(solution)/shard_map/all_gather | solution.py:142
  10.0 250.3 %all-gather.16.cloned.1.call-start = ((), (), s32[]{:S(2)}) async-start(), calls=%async_computation.16 | async-start | bytes 5308416 | tf_op jit(solution)/shard_map/all_gather | solution.py:161
  10.6 329.5 %all-gather.18.cloned.1.call-start = ((), (), s32[]{:S(2)}) async-start(), calls=%async_computation.17 | async-start | bytes 5308416 | tf_op jit(solution)/shard_map/all_gather | solution.py:163
  11.2 409.1 %reduce-scatter.25.cloned.1.call-start = ((), (), s32[]{:S(2)}) async-start(), calls=%async_computation.24 | async-start | bytes 2654208 | tf_op jit(solution)/shard_map/reduce_scatter | solution.py:288
  60.2 37.8 %copy-start.31 = (f32[768]{0:T(1024)}, f32[768]{0:T(1024)S(1)}, u32[]{:S(2)}) copy-start(f32[768]{0:T(1024)S(1)} %convert_element_type.251) | copy-start | bytes 9220
  60.2 37.8 %copy-start.24 = (f32[768]{0:T(1024)}, f32[768]{0:T(1024)S(1)}, u32[]{:S(2)}) copy-start(f32[768]{0:T(1024)S(1)} %convert_element_type.250) | copy-start | bytes 9220
  98.3 44.5 %copy-start.16 = (bf16[256,768]{0,1:T(8,128)(2,1)}, bf16[256,768]{0,1:T(8,128)(2,1)S(1)}, u32[]{:S(2)}) copy-start(bf16[256,768]{0,1:T(8,128)(2,1)S(1)} %copy.60) | copy-start | bytes 1179652
  340.1 6.2 copy-start.8
  340.1 6.2 copy-start.28
  340.1 6.2 copy-start.43
  340.1 6.2 copy-start.49
  340.1 6.2 copy-start.56
  352.3 140.5 %reduce-scatter.21.cloned.1.call-start = ((), (), s32[]{:S(2)}) async-start(), calls=%async_computation.22 | async-start | bytes 2654208 | tf_op jit(solution)/shard_map/reduce_scatter | solution.py:286
  357.0 3.3 copy-start.1
  357.0 3.3 copy-start.25
  357.0 3.3 copy-start.32
  357.0 3.3 copy-start.35
  357.0 3.3 copy-start.39
  362.4 202.7 %reduce-scatter.17.cloned.1.call-start = ((), (), s32[]{:S(2)}) async-start(), calls=%async_computation.20 | async-start | bytes 2654208 | tf_op jit(solution)/shard_map/reduce_scatter | solution.py:285
  364.7 3.5 copy-start.18
  366.0 3.5 copy-start.2
  366.0 3.5 copy-start.26
  366.0 3.5 copy-start.33
  366.1 3.5 copy-start.36
  366.1 3.5 copy-start.40
  371.8 265.5 %reduce-scatter.13.cloned.1.call-start = ((), (), s32[]{:S(2)}) async-start(), calls=%async_computation.18 | async-start | bytes 2654208 | tf_op jit(solution)/shard_map/reduce_scatter | solution.py:283
  374.4 8.9 copy-start.15
  376.6 425.7 %reduce-scatter.29.cloned.1.call-start = ((), (), s32[]{:S(2)}) async-start(), calls=%async_computation.26 | async-start | bytes 10616832 | tf_op jit(solution)/shard_map/reduce_scatter | solution.py:195
  383.3 585.0 %reduce-scatter.33.cloned.1.call-start = ((), (), s32[]{:S(2)}) async-start(), calls=%async_computation.28 | async-start | bytes 10616832 | tf_op jit(solution)/shard_map/reduce_scatter | solution.py:197
  391.0 252.6 %copy-start.55 = (bf16[768]{0:T(1024)(128)(2,1)S(1)}, bf16[768]{0:T(1024)(128)(2,1)}, u32[]{:S(2)}) copy-start(bf16[768]{0:T(1024)(128)(2,1)} %get-tuple-element.41) | copy-start | bytes 4612
  391.0 599.2 %reduce-scatter.27.cloned.1.call-start = ((), (), s32[]{:S(2)}) async-start(), calls=%async_computation.25 | async-start | bytes 184320 | tf_op jit(solution)/shard_map/reduce_scatter | solution.py:323
  422.0 590.8 %reduce-scatter.23.cloned.1.call-start = ((), (), s32[]{:S(2)}) async-start(), calls=%async_computation.23 | async-start | bytes 184320 | tf_op jit(solution)/shard_map/reduce_scatter | solution.py:317
  494.4 541.0 %reduce-scatter.19.cloned.1.call-start = ((), (), s32[]{:S(2)}) async-start(), calls=%async_computation.21 | async-start | bytes 184320 | tf_op jit(solution)/shard_map/reduce_scatter | solution.py:314
  566.7 243.3 %copy-start.12 = (bf16[768,768]{1,0:T(8,128)(2,1)S(1)}, bf16[768,768]{1,0:T(8,128)(2,1)}, u32[]{:S(2)}) copy-start(bf16[768,768]{1,0:T(8,128)(2,1)} %all-gather.12.cloned.1.call-done) | copy-start | bytes 3538948
  566.7 491.2 %reduce-scatter.15.cloned.1.call-start = ((), (), s32[]{:S(2)}) async-start(), calls=%async_computation.19 | async-start | bytes 184320 | tf_op jit(solution)/shard_map/reduce_scatter | solution.py:308
  639.0 444.0 %reduce-scatter.31.cloned.1.call-start = ((), (), s32[]{:S(2)}) async-start(), calls=%async_computation.27 | async-start | bytes 737280 | tf_op jit(solution)/shard_map/reduce_scatter | solution.py:214
  639.7 170.3 %copy-start.14 = (bf16[12,64,256]{2,1,0:T(8,128)(2,1)S(1)}, bf16[12,64,256]{2,1,0:T(8,128)(2,1)}, u32[]{:S(2)}) copy-start(bf16[12,64,256]{2,1,0:T(8,128)(2,1)} %copy-done.13) | copy-start | bytes 1179652
  804.4 7.4 copy-start.27
  804.4 7.4 copy-start.37
  804.4 7.4 copy-start.41
  804.5 302.9 %reduce-scatter.35.cloned.1.call-start = ((), (), s32[]{:S(2)}) async-start(), calls=%async_computation.29 | async-start | bytes 737280 | tf_op jit(solution)/shard_map/reduce_scatter | solution.py:220
  810.0 3.8 copy-start.45
  811.9 158.7 %copy-start.6 = (f32[256,768]{1,0:T(8,128)S(1)}, f32[256,768]{1,0:T(8,128)}, u32[]{:S(2)}) copy-start(f32[256,768]{1,0:T(8,128)} %copy-done.5) | copy-start | bytes 2359300
  813.9 157.9 %copy-start.52 = (f32[768]{0:T(1024)S(1)}, f32[768]{0:T(1024)}, u32[]{:S(2)}) copy-start(f32[768]{0:T(1024)} %convert_element_type.268) | copy-start | bytes 9220
  (27 other events, 46.9 us)
Sparse Core Ops, SparseCore 0:
  10.2 44.1 all-gather.9
  56.5 39.7 all-gather.11
  98.5 39.8 all-gather.7
  140.4 39.7 all-gather.13
  182.3 78.0 all-gather.15
  262.4 77.6 all-gather.17
  352.4 67.8 reduce-scatter.24
  423.8 68.8 reduce-scatter.20
  496.2 68.8 reduce-scatter.16
  568.4 68.8 reduce-scatter.12
  640.9 161.3 reduce-scatter.28
  805.7 162.6 reduce-scatter.32
  971.4 18.7 reduce-scatter.26
  993.1 19.6 reduce-scatter.22
  1015.6 19.6 reduce-scatter.18
  1038.2 19.6 reduce-scatter.14
  1060.9 22.0 reduce-scatter.30
  1085.3 22.0 reduce-scatter.34
where the time goes:
time: 1120 us
  waiting for transfers between devices  822 us (73%)
  blocking collectives  155 us (14%)
  matrix products  67.7 us (6%)
  other arithmetic  30.8 us (3%)
  local copies, waits for them, and re-layouts  26.5 us (2%)
  between operations  19.6 us (2%)
    reduce_scatter x1, waiting for transfers between devices, on_device(): lax.psum_scatter(hidden_term, 'shard', scatter_dimension=0, tiled=True)  158 us
    reduce_scatter x1, waiting for transfers between devices, on_device(): lax.psum_scatter(proj_term, 'shard', scatter_dimension=0, tiled=True)  95 us
    unnamed x4, blocking collectives  91.1 us
    all_gather x1, waiting for transfers between devices, on_device(): lax.all_gather(hidden_weight, 'shard', axis=0, tiled=True)  76.3 us
    all_gather x1, waiting for transfers between devices, on_device(): lax.all_gather(proj_weight, 'shard', axis=0, tiled=True)  73.2 us
    reduce_scatter x1, waiting for transfers between devices, on_device(): lax.psum_scatter(value_term, 'shard', scatter_dimension=0, tiled=True)  70.7 us
    reduce_scatter x1, waiting for transfers between devices, on_device(): lax.psum_scatter(key_term, 'shard', scatter_dimension=0, tiled=True)  70.6 us
    reduce_scatter x1, waiting for transfers between devices, on_device(): lax.psum_scatter(query_term, 'shard', scatter_dimension=0, tiled=True)  70.5 us
  transfers between devices with their start and end apart: 18, of which 17 were waited for; matrix products, arithmetic and copies ran while one was open for 10% of the time, Pallas kernels for 0%

commit v1 on v0

v1 whole, which is shorter than its diff:
```python
import jax
import jax.numpy as jnp
from jax import lax
from jax.sharding import PartitionSpec as P

HD = 64


EPS = 1e-05
ROOT_HALF = 0.7071067811865476
INV_ROOT_TWO_PI = 0.3989422804014327


def layer_norm(tokens, norm_gain, norm_shift):
    average = jnp.mean(tokens, axis=-1, keepdims=True)
    centered = tokens - average
    inv_std = lax.rsqrt(jnp.mean(centered * centered, axis=-1, keepdims=True) + EPS)
    normed = centered * inv_std
    shaped = normed * norm_gain.astype(jnp.float32) + norm_shift.astype(jnp.float32)
    return (normed, inv_std, shaped.astype(jnp.bfloat16))


def norm_grad(upstream, normed, inv_std, norm_gain):
    scaled = upstream * norm_gain.astype(jnp.float32)
    inner = (
        scaled
        - jnp.mean(scaled, axis=-1, keepdims=True)
        - normed * jnp.mean(scaled * normed, axis=-1, keepdims=True)
    )
    return (inner * inv_std, jnp.sum(upstream * normed, axis=0), jnp.sum(upstream, axis=0))


def matmul(left, right):
    return jnp.dot(left, right, preferred_element_type=jnp.float32)


def times_transposed(left, right):
    return lax.dot_general(
        left, right, (((1,), (1,)), ((), ())), preferred_element_type=jnp.float32
    )


def token_sum(left, right):
    return lax.dot_general(
        left, right, (((0,), (0,)), ((), ())), preferred_element_type=jnp.float32
    )


def gelu_parts(before):
    normal_cdf = 0.5 * (1.0 + lax.erf(before * ROOT_HALF))
    return (
        before * normal_cdf,
        normal_cdf + before * INV_ROOT_TWO_PI * jnp.exp(-0.5 * before * before),
    )


def attend(query, keys, values):
    factor = query.shape[-1] ** (-0.5)
    scores = jnp.einsum("clhd,cmhd->chlm", query, keys, preferred_element_type=jnp.float32) * factor
    row_top = jnp.max(scores, axis=-1, keepdims=True)
    log_total = row_top + jnp.log(jnp.sum(jnp.exp(scores - row_top), axis=-1, keepdims=True))
    weights = jnp.exp(scores - log_total).astype(jnp.bfloat16)
    mixed = jnp.einsum(
        "chlm,cmhd->clhd", weights, values, preferred_element_type=jnp.float32
    ).astype(jnp.bfloat16)
    return (mixed, log_total)


def attend_grad(query, keys, values, mixed, log_total, grad_mixed):
    factor = query.shape[-1] ** (-0.5)
    scores = jnp.einsum("clhd,cmhd->chlm", query, keys, preferred_element_type=jnp.float32) * factor
    weights = jnp.exp(scores - log_total)
    weights_low = weights.astype(jnp.bfloat16)
    grad_values = jnp.einsum(
        "chlm,clhd->cmhd", weights_low, grad_mixed, preferred_element_type=jnp.float32
    )
    grad_weights = jnp.einsum(
        "clhd,cmhd->chlm", grad_mixed, values, preferred_element_type=jnp.float32
    )
    delta = jnp.sum(grad_mixed.astype(jnp.float32) * mixed.astype(jnp.float32), axis=-1)
    delta = jnp.transpose(delta, (0, 2, 1))[..., None]
    grad_scores = (weights * (grad_weights - delta)).astype(jnp.bfloat16)
    grad_query = (
        jnp.einsum("chlm,cmhd->clhd", grad_scores, keys, preferred_element_type=jnp.float32)
        * factor
    )
    grad_keys = (
        jnp.einsum("chlm,clhd->cmhd", grad_scores, query, preferred_element_type=jnp.float32)
        * factor
    )
    return (grad_query, grad_keys, grad_values)


def cut_columns(matrix, likes, flat=True):
    pieces = []
    start = 0
    for like in likes:
        width = like.shape[-1]
        piece = matrix[:, start : start + width]
        pieces.append(piece.reshape(-1) if flat else piece)
        start += width
    return tuple(pieces)


def on_device(
    block_input,
    attn_gain,
    attn_shift,
    query_weight,
    query_bias,
    key_weight,
    value_weight,
    value_bias,
    out_weight,
    out_bias,
    mlp_gain,
    mlp_shift,
    hidden_weight,
    hidden_bias,
    proj_weight,
    proj_bias,
    out_cotangent,
):
    clip_count, frame_count, model_width = block_input.shape
    head_count = model_width // HD
    token_count = clip_count * frame_count

    def split_heads(matrix):
        return matrix.reshape(clip_count, frame_count, head_count, HD)

    def join_heads(tensor):
        return tensor.reshape(token_count, model_width)

    residual = block_input.reshape(token_count, model_width)
    vectors = (
        attn_gain,
        attn_shift,
        query_bias,
        value_bias,
        out_bias,
        mlp_gain,
        mlp_shift,
        proj_bias,
        hidden_bias,
    )
    squares = (query_weight, key_weight, value_weight, out_weight, hidden_weight)
    vectors_all = lax.all_gather(jnp.concatenate(vectors), "shard", axis=0, tiled=False)
    squares_all = lax.all_gather(jnp.concatenate(squares, axis=1), "shard", axis=0, tiled=True)
    proj_all = lax.all_gather(proj_weight, "shard", axis=0, tiled=True)
    (
        attn_gain_all,
        attn_shift_all,
        query_bias_all,
        value_bias_all,
        out_bias_all,
        mlp_gain_all,
        mlp_shift_all,
        proj_bias_all,
        hidden_bias_all,
    ) = cut_columns(vectors_all, vectors)
    query_all, key_all, value_all, out_all, hidden_all = cut_columns(squares_all, squares, False)
    normed_one, inv_one, input_low = layer_norm(residual, attn_gain_all, attn_shift_all)
    query_low = (matmul(input_low, query_all) + query_bias_all.astype(jnp.float32)).astype(
        jnp.bfloat16
    )
    keys_low = matmul(input_low, key_all).astype(jnp.bfloat16)
    values_low = (matmul(input_low, value_all) + value_bias_all.astype(jnp.float32)).astype(
        jnp.bfloat16
    )
    mixed, log_total = attend(
        split_heads(query_low), split_heads(keys_low), split_heads(values_low)
    )
    mixed_rows = join_heads(mixed)
    middle = residual + matmul(mixed_rows, out_all) + out_bias_all.astype(jnp.float32)
    normed_two, inv_two, middle_low = layer_norm(middle, mlp_gain_all, mlp_shift_all)
    before_act = matmul(middle_low, hidden_all) + hidden_bias_all.astype(jnp.float32)
    activated, slope = gelu_parts(before_act)
    act_low = activated.astype(jnp.bfloat16)
    block_output = middle + matmul(act_low, proj_all) + proj_bias_all.astype(jnp.float32)
    upstream = out_cotangent.reshape(token_count, model_width)
    up_low = upstream.astype(jnp.bfloat16)
    proj_term = token_sum(act_low, up_low)
    proj_bias_term = jnp.sum(upstream, axis=0)
    grad_before = times_transposed(up_low, proj_all) * slope
    before_low = grad_before.astype(jnp.bfloat16)
    hidden_term = token_sum(middle_low, before_low)
    hidden_bias_term = jnp.sum(grad_before, axis=0)
    grad_normed_two = times_transposed(before_low, hidden_all)
    grad_middle_norm, mlp_gain_term, mlp_shift_term = norm_grad(
        grad_normed_two, normed_two, inv_two, mlp_gain_all
    )
    grad_middle = upstream + grad_middle_norm
    middle_grad_low = grad_middle.astype(jnp.bfloat16)
    out_term = token_sum(mixed_rows, middle_grad_low)
    out_bias_term = jnp.sum(grad_middle, axis=0)
    grad_mixed = times_transposed(middle_grad_low, out_all).astype(jnp.bfloat16)
    grad_query, grad_keys, grad_values = attend_grad(
        split_heads(query_low),
        split_heads(keys_low),
        split_heads(values_low),
        mixed,
        log_total,
        split_heads(grad_mixed),
    )
    grad_query = join_heads(grad_query)
    grad_keys = join_heads(grad_keys)
    grad_values = join_heads(grad_values)
    query_bias_term = jnp.sum(grad_query, axis=0)
    value_bias_term = jnp.sum(grad_values, axis=0)
    query_grad_low = grad_query.astype(jnp.bfloat16)
    key_grad_low = grad_keys.astype(jnp.bfloat16)
    value_grad_low = grad_values.astype(jnp.bfloat16)
    query_term = token_sum(input_low, query_grad_low)
    key_term = token_sum(input_low, key_grad_low)
    value_term = token_sum(input_low, value_grad_low)
    grad_normed_one = (
        times_transposed(query_grad_low, query_all)
        + times_transposed(key_grad_low, key_all)
        + times_transposed(value_grad_low, value_all)
    )
    grad_input_norm, attn_gain_term, attn_shift_term = norm_grad(
        grad_normed_one, normed_one, inv_one, attn_gain_all
    )
    input_grad = grad_middle + grad_input_norm
    shards = lax.axis_size("shard")
    vector_terms = jnp.concatenate(
        [
            term.reshape(shards, -1)
            for term in (
                attn_gain_term,
                attn_shift_term,
                query_bias_term,
                value_bias_term,
                out_bias_term,
                mlp_gain_term,
                mlp_shift_term,
                proj_bias_term,
                hidden_bias_term,
            )
        ],
        axis=1,
    )
    square_terms = jnp.concatenate(
        [
            term.astype(jnp.bfloat16)
            for term in (query_term, key_term, value_term, out_term, hidden_term)
        ],
        axis=1,
    )
    vector_owned = lax.psum(vector_terms, ("rep", "shard"))
    vector_owned = lax.dynamic_index_in_dim(
        vector_owned, lax.axis_index("shard"), 0, keepdims=False
    )
    square_owned = lax.psum_scatter(square_terms, "shard", scatter_dimension=0, tiled=True)
    proj_owned = lax.psum_scatter(
        proj_term.astype(jnp.bfloat16), "shard", scatter_dimension=0, tiled=True
    )
    square_owned = lax.psum(square_owned, "rep").astype(jnp.float32)
    proj_weight_grad = lax.psum(proj_owned, "rep").astype(jnp.float32)
    (
        attn_gain_grad,
        attn_shift_grad,
        query_bias_grad,
        value_bias_grad,
        out_bias_grad,
        mlp_gain_grad,
        mlp_shift_grad,
        proj_bias_grad,
        hidden_bias_grad,
    ) = cut_columns(vector_owned[None, :], vectors)
    (
        query_weight_grad,
        key_weight_grad,
        value_weight_grad,
        out_weight_grad,
        hidden_weight_grad,
    ) = cut_columns(square_owned, squares, False)
    return (
        block_output.reshape(clip_count, frame_count, model_width),
        input_grad.reshape(clip_count, frame_count, model_width),
        attn_gain_grad,
        attn_shift_grad,
        query_weight_grad,
        query_bias_grad,
        key_weight_grad,
        value_weight_grad,
        value_bias_grad,
        out_weight_grad,
        out_bias_grad,
        mlp_gain_grad,
        mlp_shift_grad,
        hidden_weight_grad,
        hidden_bias_grad,
        proj_weight_grad,
        proj_bias_grad,
    )


def solution(mesh):
    placed = (
        P(("rep", "shard"), None, None),
        P("shard"),
        P("shard"),
        P("shard", None),
        P("shard"),
        P("shard", None),
        P("shard", None),
        P("shard"),
        P("shard", None),
        P("shard"),
        P("shard"),
        P("shard"),
        P("shard", None),
        P("shard"),
        P("shard", None),
        P("shard"),
        P(("rep", "shard"), None, None),
    )
    return jax.shard_map(
        on_device,
        mesh=mesh,
        in_specs=placed,
        out_specs=(
            P(("rep", "shard"), None, None),
            P(("rep", "shard"), None, None),
            P("shard"),
            P("shard"),
            P("shard", None),
            P("shard"),
            P("shard", None),
            P("shard", None),
            P("shard"),
            P("shard", None),
            P("shard"),
            P("shard"),
            P("shard"),
            P("shard", None),
            P("shard"),
            P("shard", None),
            P("shard"),
        ),
        check_vma=False,
    )
```

time: 1120 us -> 557 us (0.50)
  waiting for transfers between devices: 822 us -> 347 us
  blocking collectives: 155 us -> 73.9 us
  local copies, waits for them, and re-layouts: 26.5 us -> 51.4 us
  other arithmetic: 30.8 us -> 10.7 us
    reduce_scatter x12 -> x2, waiting for transfers between devices: 591 us -> 150 us  [the longest x1 150 us: on_device(): lax.psum_scatter(square_terms, 'shard', scatter_dimension=0, tiled=True)]
    unnamed x4 -> x0, blocking collectives: 91.1 us -> none
    all_gather x6 -> x2, waiting for transfers between devices: 228 us -> 157 us  [the longest x1 101 us: on_device(): lax.all_gather(jnp.concatenate(squares, axis=1), 'shard', axis=0, tiled=T...]
    psum x0 -> x1, blocking collectives: none -> 40.4 us  [on_device(): vector_owned = lax.psum(vector_terms, ('rep', 'shard'))]
    psum x0 -> x1, waiting for transfers between devices: none -> 39.8 us  [on_device(): square_owned = lax.psum(square_owned, 'rep').astype(jnp.float32)]
    all_gather x7 -> x1, blocking collectives: 63.5 us -> 33.4 us  [on_device(): lax.all_gather(jnp.concatenate(vectors), 'shard', axis=0, tiled=False)]
    convert_element_type x28 -> x1, other arithmetic: 22.5 us -> 1.09 us  [on_device(): proj_weight_grad = lax.psum(proj_owned, 'rep').astype(jnp.float32)]
    convert_element_type x0 -> x13, local copies, waits for them, and re-layouts: none -> 11.5 us  [the longest x4 7.97 us: on_device(): term.astype(jnp.bfloat16)]
  transfers between devices with their start and end apart: 18 -> 5, of which waited for: 17 -> 4; matrix products, arithmetic and copies ran while one was open for 10% -> 18% of each run, Pallas kernels for 0% -> 0%
where the time goes in v1:
time: 557 us; the launch traced here: 556 us
  waiting for transfers between devices  347 us (62%)
  blocking collectives  73.9 us (13%)
  matrix products  57.4 us (10%)
  local copies, waits for them, and re-layouts  51.4 us (9%)
  between operations  14.5 us (3%)
  other arithmetic  10.7 us (2%)
    reduce_scatter x1, waiting for transfers between devices, on_device(): lax.psum_scatter(square_terms, 'shard', scatter_dimension=0, tiled=True)  150 us
    all_gather x1, waiting for transfers between devices, on_device(): lax.all_gather(jnp.concatenate(squares, axis=1), 'shard', axis=0, tiled=T...  101 us
    all_gather x1, waiting for transfers between devices, on_device(): proj_all = lax.all_gather(proj_weight, 'shard', axis=0, tiled=True)  56 us
    psum x1, blocking collectives, on_device(): vector_owned = lax.psum(vector_terms, ('rep', 'shard'))  40.4 us
    psum x1, waiting for transfers between devices, on_device(): square_owned = lax.psum(square_owned, 'rep').astype(jnp.float32)  39.8 us
    all_gather x1, blocking collectives, on_device(): lax.all_gather(jnp.concatenate(vectors), 'shard', axis=0, tiled=False)  33.4 us
    dot_general x6, matrix products, times_transposed(): lax.dot_general(left, right, (((1,), (1,)), ((), ())), preferred_element_...  20.2 us
    unnamed x138, local copies, waits for them, and re-layouts  17.6 us
  transfers between devices with their start and end apart: 5, of which 4 were waited for; matrix products, arithmetic and copies ran while one was open for 18% of the time, Pallas kernels for 0%

profile of v1, /device:TPU:0, one launch (start us, length us, event | category | flops | bytes accessed | tf_op | source)
XLA Modules:
  0.0 555.6 jit_solution(15415747082169291236)
XLA Ops:
  14.3 33.4 %all-gather.1 = bf16[8,1,1152]{2,1,0:T(2,128)(2,1)S(1)} all-gather(bf16[1,1,1152]{2,1,0:T(2,128)(2,1)S(1)} %reshape.446), channel_id=2, replica_groups=mesh['rep'=4,'shard'=8] {'shard'}, dimensions={0}, use_global_device_ids=true | all-gather | bytes 20736 | tf_op jit(solution)/shard_map/all_gather | solution.py:147
  52.7 101.0 %all-gather.5.cloned.1.call-done = bf16[768,6144]{1,0:T(8,128)(2,1)} async-done(((bf16[96,6144]{1,0:T(8,128)(2,1)}), bf16[768,6144]{1,0:T(8,128)(2,1)}) %all-gather.5.cloned.1.call-update) | async-done | bytes 9437200 | tf_op jit(solution)/shard_map/all_gather | solution.py:148
  153.7 1.7 fusion.17
  156.4 1.7 convolution_convert_fusion.8
  158.3 1.9 fusion.16
  161.1 1.8 multiply_reduce_fusion
  164.3 1.2 copy-done.28
  166.7 3.3 multiply_convert_fusion.1
  170.1 1.2 copy-done.19
  171.3 3.7 fusion.47
  175.3 2.1 fusion.31
  177.4 56.0 %all-gather.7.cloned.1.call-done = bf16[3072,768]{1,0:T(8,128)(2,1)} async-done(((bf16[384,768]{1,0:T(8,128)(2,1)}), bf16[3072,768]{1,0:T(8,128)(2,1)}) %all-gather.7.cloned.1.call-update) | async-done | bytes 4718608 | tf_op jit(solution)/shard_map/all_gather | solution.py:149
  233.4 6.1 %fusion.45 = (f32[3072]{0:T(1024)}, bf16[256,3072]{1,0:T(8,128)(2,1)S(1)}) fusion(f32[256,3072]{1,0:T(8,128)} %get-tuple-element.58, bf16[3072,768]{1,0:T(8,128)(2,1)} %all-gather.7.cloned.1.call-done, f32[1,256,768]{2,1,0:T(8,128)} %param.33), kind=kOutput, calls=%fused_computation.119 | convolution fusion | flops 1216607232 | bytes 10235904 | tf_op jit(solution)/shard_map/dot_general | solution.py:38
  239.5 5.2 multiply_reduce_fusion.1
  246.5 2.5 convolution_convert_fusion.6
  249.1 1.9 copy.70
  251.0 2.0 copy.71
  253.0 2.7 convolution_convert_fusion.5
  255.7 2.4 copy.79
  258.1 2.4 fusion.42
  261.3 1.5 convolution_convert_fusion.2
  262.8 2.4 copy.78
  265.2 1.3 multiply_reduce_fusion.4
  266.5 2.1 multiply_convert_fusion
  268.6 1.1 copy-done.3
  270.8 1.5 copy.77
  272.3 2.1 fusion.43
  275.1 1.5 convolution_convert_fusion.4
  276.6 1.7 copy.76
  278.4 1.1 constant_dynamic-update-slice_fusion.8
  279.5 1.2 constant_dynamic-update-slice_fusion.7
  280.7 1.2 constant_dynamic-update-slice_fusion.6
  281.9 1.2 constant_dynamic-update-slice_fusion.5
  283.1 3.8 fusion
  290.2 1.3 reshape.422
  291.5 1.3 reshape.421
  292.9 1.3 reshape.423
  294.2 1.4 reshape.419
  295.6 1.4 reshape.420
  296.9 1.8 fusion.23
  298.7 1.8 convolution_add_fusion.1
  300.6 2.8 multiply_reduce_fusion.2
  305.7 40.4 %psum.21 = f32[8,1152]{1,0:T(8,128)S(1)} all-reduce(f32[8,1152]{1,0:T(8,128)S(1)} %concatenate.14), channel_id=1, replica_groups=mesh['rep'=4,'shard'=8] {'rep','shard'}, use_global_device_ids=true, to_apply=%region_20.0 | all-reduce | flops 9216 | bytes 73728 | tf_op jit(solution)/shard_map/psum | solution.py:250
  347.5 149.5 %reduce-scatter.3.cloned.1.call-done = bf16[96,6144]{1,0:T(8,128)(2,1)} async-done(((bf16[768,6144]{1,0:T(8,128)(2,1)}), bf16[96,6144]{1,0:T(8,128)(2,1)}) %reduce-scatter.3.cloned.1.call-update) | async-done | bytes 1179664 | tf_op jit(solution)/shard_map/reduce_scatter | solution.py:254
  498.4 1.8 add_bitcast_fusion
  500.2 4.6 fusion.15
  504.8 39.8 %all-reduce.3.cloned.1.call-done = (bf16[96,6144]{1,0:T(8,128)(2,1)}, bf16[384,768]{1,0:T(8,128)(2,1)}) async-done(((bf16[96,6144]{1,0:T(8,128)(2,1)}, bf16[384,768]{1,0:T(8,128)(2,1)}), (bf16[96,6144]{1,0:T(8,128)(2,1)}, bf16[384,768]{1,0:T(8,128)(2,1)})) %all-reduce.3.cloned.1.call-update) | async-done | bytes 1769488 | tf_op jit(solution)/shard_map/psum | solution.py:258
  544.6 2.3 slice.130
  (186 shorter events, 31.4 us)
Async XLA Ops:
  7.2 6.9 %copy-start.61 = (bf16[96]{0:T(256)(128)(2,1)S(1)}, bf16[96]{0:T(256)(128)(2,1)}, u32[]{:S(2)}) copy-start(bf16[96]{0:T(256)(128)(2,1)} %param.32) | copy-start | bytes 580
  7.2 6.9 %copy-start.53 = (bf16[384]{0:T(512)(128)(2,1)S(1)}, bf16[384]{0:T(512)(128)(2,1)}, u32[]{:S(2)}) copy-start(bf16[384]{0:T(512)(128)(2,1)} %param.30) | copy-start | bytes 2308
  7.2 6.9 %copy-start.60 = (bf16[96]{0:T(256)(128)(2,1)S(1)}, bf16[96]{0:T(256)(128)(2,1)}, u32[]{:S(2)}) copy-start(bf16[96]{0:T(256)(128)(2,1)} %param.28) | copy-start | bytes 580
  7.2 6.9 %copy-start.59 = (bf16[96]{0:T(256)(128)(2,1)S(1)}, bf16[96]{0:T(256)(128)(2,1)}, u32[]{:S(2)}) copy-start(bf16[96]{0:T(256)(128)(2,1)} %param.27) | copy-start | bytes 580
  7.2 6.9 %copy-start.58 = (bf16[96]{0:T(256)(128)(2,1)S(1)}, bf16[96]{0:T(256)(128)(2,1)}, u32[]{:S(2)}) copy-start(bf16[96]{0:T(256)(128)(2,1)} %param.26) | copy-start | bytes 580
  7.2 6.9 %copy-start.57 = (bf16[96]{0:T(256)(128)(2,1)S(1)}, bf16[96]{0:T(256)(128)(2,1)}, u32[]{:S(2)}) copy-start(bf16[96]{0:T(256)(128)(2,1)} %param.24) | copy-start | bytes 580
  7.3 6.9 %copy-start.56 = (bf16[96]{0:T(256)(128)(2,1)S(1)}, bf16[96]{0:T(256)(128)(2,1)}, u32[]{:S(2)}) copy-start(bf16[96]{0:T(256)(128)(2,1)} %param.21) | copy-start | bytes 580
  7.3 6.9 %copy-start.55 = (bf16[96]{0:T(256)(128)(2,1)S(1)}, bf16[96]{0:T(256)(128)(2,1)}, u32[]{:S(2)}) copy-start(bf16[96]{0:T(256)(128)(2,1)} %param.19) | copy-start | bytes 580
  7.3 6.9 %copy-start.54 = (bf16[96]{0:T(256)(128)(2,1)S(1)}, bf16[96]{0:T(256)(128)(2,1)}, u32[]{:S(2)}) copy-start(bf16[96]{0:T(256)(128)(2,1)} %param.18) | copy-start | bytes 580
  7.3 44.0 %copy-start = (f32[1,256,768]{2,1,0:T(8,128)S(1)}, f32[1,256,768]{2,1,0:T(8,128)}, u32[]{:S(2)}) copy-start(f32[1,256,768]{2,1,0:T(8,128)} %param.17) | copy-start | bytes 2359300
  7.3 146.4 %all-gather.5.cloned.1.call-start = ((), (), s32[]{:S(2)}) async-start(), calls=%async_computation.2 | async-start | bytes 10616832 | tf_op jit(solution)/shard_map/all_gather | solution.py:148
  13.3 220.2 %all-gather.7.cloned.1.call-start = ((), (), s32[]{:S(2)}) async-start(), calls=%async_computation.3 | async-start | bytes 5308416 | tf_op jit(solution)/shard_map/all_gather | solution.py:149
  14.0 333.5 %reduce-scatter.5.cloned.1.call-start = ((), (), s32[]{:S(2)}) async-start(), calls=%async_computation.5 | async-start | bytes 5308416 | tf_op jit(solution)/shard_map/reduce_scatter | solution.py:255
  49.7 108.4 %copy-start.33 = (f32[768]{0:T(1024)}, f32[768]{0:T(1024)S(1)}, u32[]{:S(2)}) copy-start(f32[768]{0:T(1024)S(1)} %reshape.435) | copy-start | bytes 9220
  50.4 107.7 %copy-start.35 = (f32[768]{0:T(1024)}, f32[768]{0:T(1024)S(1)}, u32[]{:S(2)}) copy-start(f32[768]{0:T(1024)S(1)} %reshape.436) | copy-start | bytes 9220
  158.3 4.7 copy-start.25
  161.1 4.3 copy-start.28
  166.4 3.7 copy-start.10
  166.4 3.6 copy-start.44
  166.7 3.4 copy-start.47
  166.7 4.6 copy-start.7
  175.0 322.0 %reduce-scatter.3.cloned.1.call-start = ((), (), s32[]{:S(2)}) async-start(), calls=%async_computation.4 | async-start | bytes 10616832 | tf_op jit(solution)/shard_map/reduce_scatter | solution.py:254
  233.4 6.1 %copy-start.11 = (f32[256,768]{1,0:T(8,128)S(1)}, f32[256,768]{1,0:T(8,128)}, u32[]{:S(2)}) copy-start(f32[256,768]{1,0:T(8,128)} %copy-done.10) | copy-start | bytes 2359300
  233.4 6.1 %copy-start.39 = (f32[768]{0:T(1024)S(1)}, f32[768]{0:T(1024)}, u32[]{:S(2)}) copy-start(f32[768]{0:T(1024)} %reshape.440) | copy-start | bytes 9220
  233.4 6.1 %copy-start.45 = (f32[256]{0:T(256)S(1)}, f32[256]{0:T(256)}, u32[]{:S(2)}) copy-start(f32[256]{0:T(256)} %copy-done.44) | copy-start | bytes 3076
  233.4 6.1 %copy-start.48 = (f32[256]{0:T(256)S(1)}, f32[256]{0:T(256)}, u32[]{:S(2)}) copy-start(f32[256]{0:T(256)} %copy-done.47) | copy-start | bytes 3076
  239.5 5.2 copy-start.62
  239.5 5.2 copy-start.8
  265.2 4.6 copy-start.26
  266.5 3.8 copy-start.14
  270.3 4.0 copy-start.21
  276.6 4.1 copy-start.17
  278.3 3.5 copy-start.16
  279.5 3.6 copy-start.12
  279.5 3.6 copy-start.40
  279.5 3.6 copy-start.46
  279.5 3.6 copy-start.49
  279.5 3.6 copy-start.51
  279.5 3.6 copy-start.63
  286.9 10.0 %copy-start.24 = (bf16[1,256,12,64]{1,3,2,0:T(8,128)(2,1)S(1)}, bf16[1,256,12,64]{1,3,2,0:T(8,128)(2,1)}, u32[]{:S(2)}) copy-start(bf16[1,256,12,64]{1,3,2,0:T(8,128)(2,1)} %copy-done.23) | copy-start | bytes 1179652
  287.0 11.8 %copy-start.22 = (bf16[12,64,256]{2,1,0:T(8,128)(2,1)S(1)}, bf16[12,64,256]{2,1,0:T(8,128)(2,1)}, u32[]{:S(2)}) copy-start(bf16[12,64,256]{2,1,0:T(8,128)(2,1)} %copy-done.21) | copy-start | bytes 1179652
  287.0 257.6 %all-reduce.3.cloned.1.call-start = ((), (), s32[]{:S(2)}) async-start(), calls=%async_computation.6 | async-start | bytes 3538944 | tf_op jit(solution)/shard_map/psum | solution.py:258
  288.1 12.5 %copy-start.2 = (f32[1,256,768]{2,1,0:T(8,128)S(1)}, f32[1,256,768]{2,1,0:T(8,128)}, u32[]{:S(2)}) copy-start(f32[1,256,768]{2,1,0:T(8,128)} %param.17) | copy-start | bytes 2359300
  288.1 12.5 %copy-start.30 = (bf16[1,256,12,64]{1,3,2,0:T(8,128)(2,1)S(1)}, bf16[1,256,12,64]{1,3,2,0:T(8,128)(2,1)}, u32[]{:S(2)}) copy-start(bf16[1,256,12,64]{1,3,2,0:T(8,128)(2,1)} %copy-done.29) | copy-start | bytes 1179652
  288.1 12.5 %copy-start.34 = (f32[768]{0:T(1024)S(1)}, f32[768]{0:T(1024)}, u32[]{:S(2)}) copy-start(f32[768]{0:T(1024)} %copy-done.33) | copy-start | bytes 9220
  300.6 197.8 %copy-start.6 = (f32[256,768]{1,0:T(8,128)S(1)}, f32[256,768]{1,0:T(8,128)}, u32[]{:S(2)}) copy-start(f32[256,768]{1,0:T(8,128)} %copy-done.5) | copy-start | bytes 2359300
  303.4 196.8 %copy-start.52 = (f32[768]{0:T(1024)S(1)}, f32[768]{0:T(1024)}, u32[]{:S(2)}) copy-start(f32[768]{0:T(1024)} %reshape.443) | copy-start | bytes 9220
  544.6 3.3 copy-start.32
  (21 other events, 40.7 us)
Sparse Core Ops, SparseCore 0:
  13.4 140.2 all-gather.4
  155.9 77.5 all-gather.6
  237.1 94.7 reduce-scatter.4
  335.3 161.7 reduce-scatter.2
  499.4 45.1 all-reduce.2

commit v2 on v1

--- a/solution.py
+++ b/solution.py
@@ -1,6 +1,10 @@
+import functools
+
 import jax
 import jax.numpy as jnp
 from jax import lax
+from jax.experimental import pallas as pl
+from jax.experimental.pallas import tpu as pltpu
 from jax.sharding import PartitionSpec as P
 
 HD = 64
@@ -89,6 +93,295 @@
         * factor
     )
     return (grad_query, grad_keys, grad_values)
+
+
+MESH = pl.DeviceIdType.MESH
+
+
+def ring_place(index, count):
+    odd = index % 2
+    return (index // 2) * (1 - odd) + (count - 1 - index // 2) * odd
+
+
+def ring_index(place, count):
+    late = place // (count // 2)
+    return 2 * place * (1 - late) + (2 * (count - 1 - place) + 1) * late
+
+
+def ring_steps(stream, count):
+    forward = count // 2 if stream % 2 == 0 else count - 1 - count // 2
+    return (forward, count - 1 - forward)
+
+
+def greet(peers):
+    barrier = pltpu.get_barrier_semaphore()
+    for peer in peers:
+        pl.semaphore_signal(barrier, inc=1, device_id=peer, device_id_type=MESH)
+    pl.semaphore_wait(barrier, len(peers))
+
+
+def remote(src, dst, send_sem, recv_sem, peer):
+    return pltpu.make_async_remote_copy(
+        src_ref=src,
+        dst_ref=dst,
+        send_sem=send_sem,
+        recv_sem=recv_sem,
+        device_id=peer,
+        device_id_type=MESH,
+    )
+
+
+def gather_kernel(count, streams, *refs):
+    own = refs[:streams]
+    whole = refs[streams : 2 * streams]
+    ring_send, ring_recv, pair_send, pair_recv, local_sem = refs[2 * streams :]
+    me = lax.axis_index("shard")
+    rep = lax.axis_index("rep")
+    core = rep % 2
+    place = ring_place(me, count)
+    ways = (
+        {"shard": ring_index((place + 1) % count, count)},
+        {"shard": ring_index((place + count - 1) % count, count)},
+    )
+    partner = {"rep": rep + 1 - 2 * core}
+    greet((*ways, partner))
+
+    def owner_from(way, step):
+        offset = count - step if way == 0 else step
+        return ring_index((place + offset) % count, count)
+
+    pending = []
+    locals_ = []
+    hops = {}
+    longest = max(max(ring_steps(i, count)) for i in range(streams))
+    for step in range(longest + 1):
+        for i in range(streams):
+            steps = ring_steps(i, count)
+            for way in range(2):
+                if step > steps[way]:
+                    continue
+                slot = way * steps[0] + step
+                if step > 0:
+                    hops[(i, way)].wait_recv()
+                    owner = owner_from(way, step)
+                    landed = whole[i].at[owner, core]
+                    cross = remote(
+                        landed, landed, pair_send.at[i, slot - 1], pair_recv.at[i, slot - 1], partner
+                    )
+                if step < steps[way]:
+                    owner = owner_from(way, step)
+                    source = own[i].at[core] if step == 0 else whole[i].at[owner, core]
+                    hop = remote(
+                        source,
+                        whole[i].at[owner, core],
+                        ring_send.at[i, slot],
+                        ring_recv.at[i, slot],
+                        ways[way],
+                    )
+                    hop.start()
+                    hops[(i, way)] = hop
+                    pending.append(hop)
+                if step > 0:
+                    cross.start()
+                    locals_.append(cross)
+        if step == 0:
+            keep = [
+                pltpu.make_async_copy(own[i], whole[i].at[me], local_sem.at[i])
+                for i in range(streams)
+            ]
+            for copy in keep:
+                copy.start()
+    for cross in locals_:
+        cross.wait()
+    for hop in pending:
+        hop.wait_send()
+    for copy in keep:
+        copy.wait()
+
+
+def gather_all(blocks):
+    count = lax.axis_size("shard")
+    streams = len(blocks)
+    halves = [block.reshape(2, -1, block.shape[-1]) for block in blocks]
+    dma = pltpu.SemaphoreType.DMA
+    outs = pl.pallas_call(
+        functools.partial(gather_kernel, count, streams),
+        out_shape=[jax.ShapeDtypeStruct((count, *half.shape), half.dtype) for half in halves],
+        in_specs=[pl.BlockSpec(memory_space=pltpu.VMEM)] * streams,
+        out_specs=[pl.BlockSpec(memory_space=pl.ANY)] * streams,
+        scratch_shapes=[dma((streams, count - 1))] * 4 + [dma((streams,))],
+        compiler_params=pltpu.CompilerParams(collective_id=0, has_side_effects=True),
+    )(*halves)
+    return [out.reshape(-1, out.shape[-1]) for out in outs]
+
+
+def reduce_kernel(count, peer_bits, streams, *refs):
+    term = refs[:streams]
+    total = refs[streams : 2 * streams]
+    pair_got = refs[2 * streams : 3 * streams]
+    ring_out = refs[3 * streams : 4 * streams]
+    ring_got = refs[4 * streams : 5 * streams]
+    rep_out = refs[5 * streams : 6 * streams]
+    rep_got = refs[6 * streams : 7 * streams]
+    (
+        pair_send,
+        pair_recv,
+        ring_send,
+        ring_recv,
+        rep_send,
+        rep_recv,
+        last_send,
+        last_recv,
+    ) = refs[7 * streams :]
+    me = lax.axis_index("shard")
+    rep = lax.axis_index("rep")
+    core = rep % 2
+    place = ring_place(me, count)
+    ways = (
+        {"shard": ring_index((place + 1) % count, count)},
+        {"shard": ring_index((place + count - 1) % count, count)},
+    )
+    partner = {"rep": rep + 1 - 2 * core}
+    across = [
+        {"rep": rep + bit * (1 - 2 * ((rep // bit) % 2))} for bit in peer_bits
+    ]
+    greet((*ways, partner, *across))
+
+    def target(way, steps, step):
+        reach = steps[way] - step
+        return ring_index((place + (reach if way == 0 else count - reach)) % count, count)
+
+    sent = []
+    crossed = {}
+    longest = max(max(ring_steps(i, count)) for i in range(streams))
+    for step in range(longest + 1):
+        for i in range(streams):
+            steps = ring_steps(i, count)
+            for way in range(2):
+                if step < steps[way]:
+                    owner, slot = target(way, steps, step), way * steps[0] + step
+                elif step == steps[0] and way == 0:
+                    owner, slot = me, count - 1
+                else:
+                    continue
+                cross = remote(
+                    term[i].at[owner, 1 - core],
+                    pair_got[i].at[owner],
+                    pair_send.at[i, slot],
+                    pair_recv.at[i, slot],
+                    partner,
+                )
+                cross.start()
+                crossed[(i, slot)] = cross
+                sent.append(cross)
+
+    def pair_sum(i, owner, slot):
+        crossed[(i, slot)].wait_recv()
+        return term[i][owner, core].astype(jnp.float32) + pair_got[i][owner].astype(jnp.float32)
+
+    hops = {}
+    for step in range(longest):
+        for i in range(streams):
+            steps = ring_steps(i, count)
+            for way in range(2):
+                if step >= steps[way]:
+                    continue
+                slot = way * steps[0] + step
+                partial = pair_sum(i, target(way, steps, step), slot)
+                if step > 0:
+                    hops[(i, way)].wait_recv()
+                    partial += ring_got[i][slot - 1].astype(jnp.float32)
+                ring_out[i][slot] = partial.astype(ring_out[i].dtype)
+                hop = remote(
+                    ring_out[i].at[slot],
+                    ring_got[i].at[slot],
+                    ring_send.at[i, slot],
+                    ring_recv.at[i, slot],
+                    ways[way],
+                )
+                hop.start()
+                hops[(i, way)] = hop
+                sent.append(hop)
+    owned = {}
+    swaps = {}
+
+    def swap(i, level):
+        rep_out[i][level] = owned[i].astype(rep_out[i].dtype)
+        move = remote(
+            rep_out[i].at[level],
+            rep_got[i].at[level],
+            rep_send.at[i, level],
+            rep_recv.at[i, level],
+            across[level],
+        )
+        move.start()
+        swaps[(i, level)] = move
+        sent.append(move)
+
+    for i in range(streams):
+        steps = ring_steps(i, count)
+        value = pair_sum(i, me, count - 1)
+        for way in range(2):
+            if steps[way]:
+                hops[(i, way)].wait_recv()
+                value += ring_got[i][way * steps[0] + steps[way] - 1].astype(jnp.float32)
+        owned[i] = value
+        if across:
+            swap(i, 0)
+    for level in range(len(across)):
+        for i in range(streams):
+            swaps[(i, level)].wait_recv()
+            owned[i] = rep_out[i][level].astype(jnp.float32) + rep_got[i][level].astype(jnp.float32)
+            if level + 1 < len(across):
+                swap(i, level + 1)
+            else:
+                total[i][core] = owned[i]
+                final = remote(
+                    total[i].at[core],
+                    total[i].at[core],
+                    last_send.at[i],
+                    last_recv.at[i],
+                    partner,
+                )
+                final.start()
+                crossed[(i, "final")] = final
+    for i in range(streams):
+        crossed[(i, "final")].wait()
+    for copy in sent:
+        copy.wait_send()
+
+
+def reduce_all(terms):
+    count = lax.axis_size("shard")
+    reps = lax.axis_size("rep")
+    peer_bits = [1 << k for k in range(1, reps.bit_length() - 1)]
+    streams = len(terms)
+    halves = [term.reshape(count, 2, -1, term.shape[-1]) for term in terms]
+    dma = pltpu.SemaphoreType.DMA
+
+    def slots(number):
+        return [pltpu.VMEM((number, *half.shape[2:]), half.dtype) for half in halves]
+
+    levels = len(peer_bits)
+    outs = pl.pallas_call(
+        functools.partial(reduce_kernel, count, peer_bits, streams),
+        out_shape=[jax.ShapeDtypeStruct(half.shape[1:], jnp.float32) for half in halves],
+        in_specs=[pl.BlockSpec(memory_space=pltpu.VMEM)] * streams,
+        out_specs=[pl.BlockSpec(memory_space=pltpu.VMEM)] * streams,
+        scratch_shapes=slots(count)
+        + slots(count - 1)
+        + slots(count - 1)
+        + slots(levels)
+        + slots(levels)
+        + [dma((streams, count))] * 2
+        + [dma((streams, count - 1))] * 2
+        + [dma((streams, levels))] * 2
+        + [dma((streams,))] * 2,
+        compiler_params=pltpu.CompilerParams(
+            collective_id=1, has_side_effects=True, vmem_limit_bytes=60 * 1024 * 1024
+        ),
+    )(*halves)
+    return [out.reshape(-1, out.shape[-1]) for out in outs]
 
 
 def cut_columns(matrix, likes, flat=True):
@@ -143,10 +436,16 @@
         proj_bias,
         hidden_bias,
     )
-    squares = (query_weight, key_weight, value_weight, out_weight, hidden_weight)
-    vectors_all = lax.all_gather(jnp.concatenate(vectors), "shard", axis=0, tiled=False)
-    squares_all = lax.all_gather(jnp.concatenate(squares, axis=1), "shard", axis=0, tiled=True)
-    proj_all = lax.all_gather(proj_weight, "shard", axis=0, tiled=True)
+    squares = (query_weight, key_weight, value_weight, out_weight)
+    squares_all, hidden_all, proj_all, vectors_all = gather_all(
+        (
+            jnp.concatenate(squares, axis=1),
+            hidden_weight,
+            proj_weight,
+            jnp.concatenate(vectors).reshape(2, -1),
+        )
+    )
+    vectors_all = vectors_all.reshape(lax.axis_size("shard"), -1)
     (
         attn_gain_all,
         attn_shift_all,
@@ -158,7 +457,7 @@
         proj_bias_all,
         hidden_bias_all,
     ) = cut_columns(vectors_all, vectors)
-    query_all, key_all, value_all, out_all, hidden_all = cut_columns(squares_all, squares, False)
+    query_all, key_all, value_all, out_all = cut_columns(squares_all, squares, False)
     normed_one, inv_one, input_low = layer_norm(residual, attn_gain_all, attn_shift_all)
     query_low = (matmul(input_low, query_all) + query_bias_all.astype(jnp.float32)).astype(
         jnp.bfloat16
@@ -243,20 +542,18 @@
     square_terms = jnp.concatenate(
         [
             term.astype(jnp.bfloat16)
-            for term in (query_term, key_term, value_term, out_term, hidden_term)
+            for term in (query_term, key_term, value_term, out_term)
         ],
         axis=1,
     )
-    vector_owned = lax.psum(vector_terms, ("rep", "shard"))
-    vector_owned = lax.dynamic_index_in_dim(
-        vector_owned, lax.axis_index("shard"), 0, keepdims=False
-    )
-    square_owned = lax.psum_scatter(square_terms, "shard", scatter_dimension=0, tiled=True)
-    proj_owned = lax.psum_scatter(
-        proj_term.astype(jnp.bfloat16), "shard", scatter_dimension=0, tiled=True
-    )
-    square_owned = lax.psum(square_owned, "rep").astype(jnp.float32)
-    proj_weight_grad = lax.psum(proj_owned, "rep").astype(jnp.float32)
+    square_owned, hidden_weight_grad, proj_weight_grad, vector_owned = reduce_all(
+        (
+            square_terms,
+            hidden_term.astype(jnp.bfloat16),
+            proj_term.astype(jnp.bfloat16),
+            vector_terms.reshape(2 * shards, -1),
+        )
+    )
     (
         attn_gain_grad,
         attn_shift_grad,
@@ -267,13 +564,12 @@
         mlp_shift_grad,
         proj_bias_grad,
         hidden_bias_grad,
-    ) = cut_columns(vector_owned[None, :], vectors)
+    ) = cut_columns(vector_owned.reshape(1, -1), vectors)
     (
         query_weight_grad,
         key_weight_grad,
         value_weight_grad,
         out_weight_grad,
-        hidden_weight_grad,
     ) = cut_columns(square_owned, squares, False)
     return (
         block_output.reshape(clip_count, frame_count, model_width),

time: 557 us -> 288 us (0.52)
  waiting for transfers between devices: 347 us -> 0 us
  Pallas kernels: 0 us -> 179 us
  blocking collectives: 73.9 us -> 0 us
  between operations: 14.5 us -> 1.34 us
  matrix products: 57.4 us -> 44.8 us
  local copies, waits for them, and re-layouts: 51.4 us -> 41.3 us
  other arithmetic: 10.7 us -> 20.2 us
    pallas_call x0 -> x2, Pallas kernels: none -> 179 us  [the longest x1 100 us: reduce_all(): pl.pallas_call(functools.partial(reduce_kernel, count, peer_bits, streams...]
    all_gather x2 -> x0, waiting for transfers between devices: 157 us -> none  [the longest x1 101 us: on_device(): lax.all_gather(jnp.concatenate(squares, axis=1), 'shard', axis=0, tiled=T...]
    reduce_scatter x2 -> x0, waiting for transfers between devices: 150 us -> none  [the longest x1 150 us: on_device(): lax.psum_scatter(square_terms, 'shard', scatter_dimension=0, tiled=True)]
    psum x1 -> x0, blocking collectives: 40.4 us -> none  [on_device(): vector_owned = lax.psum(vector_terms, ('rep', 'shard'))]
    psum x1 -> x0, waiting for transfers between devices: 39.8 us -> none  [on_device(): square_owned = lax.psum(square_owned, 'rep').astype(jnp.float32)]
    all_gather x1 -> x0, blocking collectives: 33.4 us -> none  [on_device(): lax.all_gather(jnp.concatenate(vectors), 'shard', axis=0, tiled=False)]
    unnamed x138 -> x100, local copies, waits for them, and re-layouts: 17.6 us -> 2.89 us
    concatenate x2, local copies, waits for them, and re-layouts: 1.2 us -> 12.9 us  [the longest x1 6.78 us: on_device(): jnp.concatenate([term.astype(jnp.bfloat16) for term in (query_term, key_t...]
  transfers between devices with their start and end apart: 5 -> 0, of which waited for: 4 -> 0; matrix products, arithmetic and copies ran while one was open for 18% -> 0% of each run, Pallas kernels for 0% -> 0%
where the time goes in v2:
time: 288 us; the launch traced here: 287 us
  Pallas kernels  179 us (62%)
  matrix products  44.8 us (16%)
  local copies, waits for them, and re-layouts  41.3 us (14%)
  other arithmetic  20.2 us (7%)
    pallas_call x1, Pallas kernels, reduce_all(): pl.pallas_call(functools.partial(reduce_kernel, count, peer_bits, streams...  100 us
    pallas_call x1, Pallas kernels, gather_all(): pl.pallas_call(functools.partial(gather_kernel, count, streams), out_shap...  78.8 us
    dot_general x6, matrix products, times_transposed(): lax.dot_general(left, right, (((1,), (1,)), ((), ())), preferred_element_...  15.2 us
    dot_general x6, matrix products, matmul(): return jnp.dot(left, right, preferred_element_type=jnp.float32)  11.8 us
    dot_general x6, matrix products, token_sum(): lax.dot_general(left, right, (((0,), (0,)), ((), ())), preferred_element_...  10.3 us
    reshape x9, local copies, waits for them, and re-layouts, on_device(): term.reshape(shards, -1)  9.42 us
    concatenate x1, local copies, waits for them, and re-layouts, on_device(): jnp.concatenate([term.astype(jnp.bfloat16) for term in (query_term, key_t...  6.78 us
    concatenate x1, local copies, waits for them, and re-layouts, on_device(): jnp.concatenate(vectors).reshape(2, -1)  6.11 us

profile of v2, /device:TPU:0, one launch (start us, length us, event | category | flops | bytes accessed | tf_op | source)
XLA Modules:
  0.0 286.8 jit_solution(13446501588125787602)
XLA Ops:
  0.7 1.3 reduce_sum.173
  2.0 1.4 multiply_reduce_fusion.7
  3.4 6.1 %concatenate.13 = bf16[1152]{0:T(1024)(128)(2,1)S(1)} concatenate(bf16[96]{0:T(256)(128)(2,1)} %param.18, bf16[96]{0:T(256)(128)(2,1)} %param.19, bf16[96]{0:T(256)(128)(2,1)} %param.21, bf16[96]{0:T(256)(128)(2,1)} %param.24, bf16[96]{0:T(256)(128)(2,1)} %param.26, bf16[96]{0:T(256)(128)(2,1)} %param.27, bf16[96]{0:T(256)(128)(2,1)} %param.28, bf16[96]{0:T(256)(128)(2,1)} %param.32, ...), dimensions={0} | concatenate | bytes 4608 | tf_op jit(solution)/shard_map/concatenate | solution.py:445
  10.2 1.2 reduce_sum.191
  12.1 2.0 pad_maximum_fusion.1
  14.0 78.8 %shard_map.296 = (bf16[8,2,48,3072]{3,2,1,0:T(8,128)(2,1)}, bf16[8,2,48,3072]{3,2,1,0:T(8,128)(2,1)}, bf16[8,2,192,768]{3,2,1,0:T(8,128)(2,1)}, bf16[8,2,1,576]{3,2,1,0:T(2,128)(2,1)}) custom-call(bf16[2,48,3072]{2,1,0:T(8,128)(2,1)} %bitcast.161, bf16[2,48,3072]{2,1,0:T(8,128)(2,1)} %bitcast.167, bf16[2,192,768]{2,1,0:T(8,128)(2,1)} %bitcast.168, ...), custom_call_target="tpu_custom_call" | custom-call | tf_op jit(solution)/shard_map/pallas_call | solution.py:207
  92.9 0.9 reduce.9
  98.0 1.7 fusion.10
  99.7 0.9 copy.51
  100.6 1.7 fusion.9
  102.4 1.7 convolution_convert_fusion.8
  104.2 0.9 copy.52
  105.1 0.9 copy.50
  106.0 1.8 multiply_reduce_fusion
  109.2 2.3 fusion.39
  111.9 1.9 multiply_convert_fusion.1
  114.4 3.0 %fusion.40 = (f32[3072]{0:T(1024)}, bf16[256,3072]{1,0:T(8,128)(2,1)S(1)}) fusion(f32[256,3072]{1,0:T(8,128)S(1)} %get-tuple-element.72, bf16[3072,768]{1,0:T(8,128)(2,1)S(1)} %bitcast.176, f32[1,256,768]{2,1,0:T(8,128)S(1)} %copy-done.6), kind=kOutput, calls=%fused_computation.110 | convolution fusion | flops 1216803840 | bytes 10235904 | tf_op jit(solution)/shard_map/dot_general | solution.py:42
  117.4 2.3 fusion.8
  119.7 3.1 %multiply_reduce_fusion.1 = (f32[768]{0:T(1024)}, f32[256]{0:T(256)}, f32[256]{0:T(256)}, f32[768]{0:T(1024)}, f32[256,768]{1,0:T(8,128)}) fusion(f32[256,768]{1,0:T(8,128)S(1)} %get-tuple-element.70, f32[256]{0:T(256)S(1)} %add_rsqrt_fusion, f32[256]{0:T(256)S(1)} %broadcast_multiply_fusion.4, f32[768]{0:T(1024)S(1)} %copy-done.26, ...), kind=kOutput, calls=%fused_computation.52 | convolution fusion | flops 1209726976 | bytes 7877632 | tf_op jit(solution)/shard_map/dot_general | solution.py:42
  122.8 1.3 reshape.471
  124.1 1.3 reshape.468
  126.1 3.4 %fusion.35 = (f32[768]{0:T(1024)}, f32[256,768]{1,0:T(8,128)}) fusion(f32[256]{0:T(256)S(1)} %get-tuple-element.79, f32[256]{0:T(256)} %copy-done.41, f32[256,768]{1,0:T(8,128)} %copy-done.3, f32[256]{0:T(256)} %copy-done.36, f32[256]{0:T(256)S(1)} %get-tuple-element.80, f32[256,768]{1,0:T(8,128)} %get-tuple-element.73, f32[768]{0:T(1024)} %reshape.489, ...), kind=kLoop, calls=%fused_computation.105 | loop fusion | flops 1768704 | bytes 3155968 | tf_op jit(solution)/shard_map/reduce_sum | solution.py:494
  129.5 1.4 reshape.467
  130.9 1.3 reshape.469
  132.2 2.8 convolution_convert_fusion.6
  135.0 1.9 copy.54
  137.0 2.0 copy.55
  139.0 1.4 multiply_reduce_fusion.4
  140.4 3.0 %fusion.37 = (f32[12,64]{1,0:T(8,128)}, bf16[1,256,12,64]{1,3,2,0:T(8,128)(2,1)}) fusion(bf16[256,12,64]{0,2,1:T(8,128)(2,1)} %bitcast.158, f32[12,256,256]{1,2,0:T(8,128)S(1)} %get-tuple-element.68, f32[12,256]{1,0:T(8,128)S(1)} %log_add_fusion), kind=kOutput, calls=%fused_computation.107 | convolution fusion | flops 103415040 | bytes 3947520 | tf_op jit(solution)/shard_map/chlm,clhd->cmhd/dot_general | solution.py:78
  143.5 0.9 multiply_convert_fusion
  147.0 1.8 fusion.16
  148.8 1.9 convolution_add_fusion.2
  150.7 2.7 multiply_reduce_fusion.2
  153.4 1.4 reshape.463
  156.1 1.9 add_bitcast_fusion
  158.5 0.7 reshape.464
  159.3 0.8 concatenate.15
  160.1 0.7 reshape_reshape.14.refs_3_
  160.8 1.5 convolution_convert_fusion.2
  163.2 2.5 pad_maximum_fusion
  165.8 6.8 %copy.60 = bf16[768,3072]{1,0:T(8,128)(2,1)} copy(bf16[768,3072]{0,1:T(8,128)(2,1)} %pad_maximum_fusion) | data formatting | bytes 9437184 | tf_op jit(solution)/shard_map/concatenate | solution.py:542
  172.7 3.7 %convolution_convert_fusion.1 = bf16[768,3072]{1,0:T(8,128)(2,1)} fusion(bf16[256,3072]{1,0:T(8,128)(2,1)S(1)} %copy-done.22, f32[256,768]{1,0:T(8,128)S(1)} %copy-done.4, f32[768]{0:T(1024)S(1)} %copy-done.29, f32[768]{0:T(1024)S(1)} %copy-done.27, f32[256]{0:T(256)S(1)} %copy-done.42, f32[256]{0:T(256)S(1)} %copy-done.37), kind=kOutput, calls=%fused_computation.1 | convolution fusion | flops 1211301888 | bytes 7086080 | tf_op jit(solution)/shard_map/dot_general | solution.py:48
  176.4 3.7 %fusion.41 = bf16[3072,768]{1,0:T(8,128)(2,1)} fusion(bf16[256,3072]{1,0:T(8,128)(2,1)S(1)} %copy-done.11, f32[1,256,768]{2,1,0:T(8,128)S(1)} %copy-done.7), kind=kOutput, calls=%fused_computation.111 | convolution fusion | flops 1207959552 | bytes 7077888 | tf_op jit(solution)/shard_map/dot_general | solution.py:48
  180.1 100.2 %shard_map.297 = (f32[2,48,3072]{2,1,0:T(8,128)}, f32[2,48,3072]{2,1,0:T(8,128)}, f32[2,192,768]{2,1,0:T(8,128)}, f32[2,1,576]{2,1,0:T(1,128)}) custom-call(bf16[8,2,48,3072]{3,2,1,0:T(8,128)(2,1)} %bitcast.137, bf16[8,2,48,3072]{3,2,1,0:T(8,128)(2,1)} %bitcast.136, bf16[8,2,192,768]{3,2,1,0:T(8,128)(2,1)} %bitcast.135, f32[8,2,1,576]{3,2,1,0:T(1,128)} %reshape_reshape.14.refs_3_), custom_call_target="tpu_custom_call" | custom-call | tf_op jit(solution)/shard_map/pallas_call | solution.py:366
  280.4 0.9 reduce.10
  281.3 2.3 fusion.36
  284.8 1.0 copy.68
  285.8 1.0 copy.69
  (137 shorter events, 15.0 us)
Async XLA Ops:
  0.7 96.9 %copy-start = (f32[1,256,768]{2,1,0:T(8,128)S(1)}, f32[1,256,768]{2,1,0:T(8,128)}, u32[]{:S(2)}) copy-start(f32[1,256,768]{2,1,0:T(8,128)} %param.17) | copy-start | bytes 2359300
  2.0 95.9 %copy-start.34 = (f32[256]{0:T(256)}, f32[256]{0:T(256)S(1)}, u32[]{:S(2)}) copy-start(f32[256]{0:T(256)S(1)} %broadcast_multiply_fusion.5) | copy-start | bytes 3076
  3.4 94.6 %copy-start.38 = (f32[256]{0:T(256)}, f32[256]{0:T(256)S(1)}, u32[]{:S(2)}) copy-start(f32[256]{0:T(256)S(1)} %add_rsqrt_fusion.1) | copy-start | bytes 3076
  96.0 6.4 %copy-start.30 = (f32[768]{0:T(1024)}, f32[768]{0:T(1024)S(1)}, u32[]{:S(2)}) copy-start(f32[768]{0:T(1024)S(1)} %reshape.484) | copy-start | bytes 9220
  106.0 2.4 copy-start.18
  107.8 1.4 copy-start.1
  107.8 1.4 copy-start.40
  107.8 4.0 %slice-start = ((s8[4718592]{0:T(1024)(128)(4,1)}), s8[4194304]{0:T(1024)(128)(4,1)S(1)}, s32[]{:S(2)}) async-start(s8[4718592]{0:T(1024)(128)(4,1)} %bitcast.170), calls=%async_computation | async-start | bytes 8388608
  108.4 3.4 %copy-start.26 = (f32[768]{0:T(1024)S(1)}, f32[768]{0:T(1024)}, u32[]{:S(2)}) copy-start(f32[768]{0:T(1024)} %reshape.489) | copy-start | bytes 9220
  108.4 3.4 %copy-start.28 = (f32[768]{0:T(1024)S(1)}, f32[768]{0:T(1024)}, u32[]{:S(2)}) copy-start(f32[768]{0:T(1024)} %reshape.490) | copy-start | bytes 9220
  108.5 3.4 %copy-start.43 = (f32[3072]{0:T(1024)S(1)}, f32[3072]{0:T(1024)}, u32[]{:S(2)}) copy-start(f32[3072]{0:T(1024)} %reshape.491) | copy-start | bytes 36868
  108.5 3.4 %slice-start.1 = ((s8[4718592]{0:T(1024)(128)(4,1)}), s8[524288]{0:T(1024)(128)(4,1)S(1)}, s32[]{:S(2)}) async-start(s8[4718592]{0:T(1024)(128)(4,1)} %bitcast.170), calls=%async_computation.1 | async-start | bytes 1048576
  109.2 2.6 copy-start.8
  111.5 8.2 %copy-start.3 = (f32[256,768]{1,0:T(8,128)}, f32[256,768]{1,0:T(8,128)S(1)}, u32[]{:S(2)}) copy-start(f32[256,768]{1,0:T(8,128)S(1)} %get-tuple-element.70) | copy-start | bytes 2359300
  111.5 8.2 %copy-start.36 = (f32[256]{0:T(256)}, f32[256]{0:T(256)S(1)}, u32[]{:S(2)}) copy-start(f32[256]{0:T(256)S(1)} %broadcast_multiply_fusion.4) | copy-start | bytes 3076
  111.6 2.5 slice-start.2
  111.9 7.9 %copy-start.41 = (f32[256]{0:T(256)}, f32[256]{0:T(256)S(1)}, u32[]{:S(2)}) copy-start(f32[256]{0:T(256)S(1)} %add_rsqrt_fusion) | copy-start | bytes 3076
  111.9 2.4 copy-start.6
  111.9 2.5 slice-start.3
  113.8 3.6 %copy-start.10 = (bf16[256,3072]{1,0:T(8,128)(2,1)}, bf16[256,3072]{1,0:T(8,128)(2,1)S(1)}, u32[]{:S(2)}) copy-start(bf16[256,3072]{1,0:T(8,128)(2,1)S(1)} %get-tuple-element.71) | copy-start | bytes 4718596
  114.4 3.0 %copy-start.44 = (f32[768]{0:T(1024)S(1)}, f32[768]{0:T(1024)}, u32[]{:S(2)}) copy-start(f32[768]{0:T(1024)} %reshape.492) | copy-start | bytes 9220
  117.4 2.3 copy-start.21
  139.0 4.5 %copy-start.19 = (bf16[256,768]{0,1:T(8,128)(2,1)S(1)}, bf16[256,768]{0,1:T(8,128)(2,1)}, u32[]{:S(2)}) copy-start(bf16[256,768]{0,1:T(8,128)(2,1)} %copy.50) | copy-start | bytes 1179652
  139.0 4.5 %copy-start.20 = (bf16[256,768]{0,1:T(8,128)(2,1)S(1)}, bf16[256,768]{0,1:T(8,128)(2,1)}, u32[]{:S(2)}) copy-start(bf16[256,768]{0,1:T(8,128)(2,1)} %copy.54) | copy-start | bytes 1179652
  143.5 1.6 copy-start.17
  144.5 1.8 copy-start.33
  145.1 3.7 %copy-start.12 = (bf16[12,64,256]{2,1,0:T(8,128)(2,1)}, bf16[12,64,256]{2,1,0:T(8,128)(2,1)S(1)}, u32[]{:S(2)}) copy-start(bf16[12,64,256]{2,1,0:T(8,128)(2,1)S(1)} %fusion.11) | copy-start | bytes 1179652
  145.6 1.4 copy-start.14
  145.6 5.1 %copy-start.2 = (f32[1,256,768]{2,1,0:T(8,128)S(1)}, f32[1,256,768]{2,1,0:T(8,128)}, u32[]{:S(2)}) copy-start(f32[1,256,768]{2,1,0:T(8,128)} %param.17) | copy-start | bytes 2359300
  145.6 5.1 %copy-start.23 = (bf16[1,256,12,64]{1,3,2,0:T(8,128)(2,1)S(1)}, bf16[1,256,12,64]{1,3,2,0:T(8,128)(2,1)}, u32[]{:S(2)}) copy-start(bf16[1,256,12,64]{1,3,2,0:T(8,128)(2,1)} %get-tuple-element.48) | copy-start | bytes 1179652
  145.6 5.1 %copy-start.31 = (f32[768]{0:T(1024)S(1)}, f32[768]{0:T(1024)}, u32[]{:S(2)}) copy-start(f32[768]{0:T(1024)} %copy-done.30) | copy-start | bytes 9220
  145.6 5.1 %copy-start.35 = (f32[256]{0:T(256)S(1)}, f32[256]{0:T(256)}, u32[]{:S(2)}) copy-start(f32[256]{0:T(256)} %copy-done.34) | copy-start | bytes 3076
  145.6 5.1 %copy-start.39 = (f32[256]{0:T(256)S(1)}, f32[256]{0:T(256)}, u32[]{:S(2)}) copy-start(f32[256]{0:T(256)} %copy-done.38) | copy-start | bytes 3076
  148.8 7.4 %copy-start.5 = (f32[256,768]{1,0:T(8,128)S(1)}, f32[256,768]{1,0:T(8,128)}, u32[]{:S(2)}) copy-start(f32[256,768]{1,0:T(8,128)} %get-tuple-element.42) | copy-start | bytes 2359300
  150.7 7.3 %copy-start.9 = (bf16[12,64,256]{2,1,0:T(8,128)(2,1)S(1)}, bf16[12,64,256]{2,1,0:T(8,128)(2,1)}, u32[]{:S(2)}) copy-start(bf16[12,64,256]{2,1,0:T(8,128)(2,1)} %copy-done.8) | copy-start | bytes 1179652
  153.4 5.9 %copy-start.32 = (f32[8,384]{1,0:T(8,128)S(1)}, f32[8,384]{1,0:T(8,128)}, u32[]{:S(2)}) copy-start(f32[8,384]{1,0:T(8,128)} %reshape.471) | copy-start | bytes 36868
  158.0 4.3 %copy-start.13 = (bf16[12,64,256]{2,1,0:T(8,128)(2,1)S(1)}, bf16[12,64,256]{2,1,0:T(8,128)(2,1)}, u32[]{:S(2)}) copy-start(bf16[12,64,256]{2,1,0:T(8,128)(2,1)} %copy-done.12) | copy-start | bytes 1179652
  158.0 4.7 %copy-start.15 = (bf16[1,256,12,64]{1,3,2,0:T(8,128)(2,1)S(1)}, bf16[1,256,12,64]{1,3,2,0:T(8,128)(2,1)}, u32[]{:S(2)}) copy-start(bf16[1,256,12,64]{1,3,2,0:T(8,128)(2,1)} %copy-done.14) | copy-start | bytes 1179652
  165.8 6.8 %copy-start.4 = (f32[256,768]{1,0:T(8,128)S(1)}, f32[256,768]{1,0:T(8,128)}, u32[]{:S(2)}) copy-start(f32[256,768]{1,0:T(8,128)} %copy-done.3) | copy-start | bytes 2359300
  165.8 6.8 %copy-start.22 = (bf16[256,3072]{1,0:T(8,128)(2,1)S(1)}, bf16[256,3072]{1,0:T(8,128)(2,1)}, u32[]{:S(2)}) copy-start(bf16[256,3072]{1,0:T(8,128)(2,1)} %copy-done.21) | copy-start | bytes 4718596
  165.8 6.8 %copy-start.27 = (f32[768]{0:T(1024)S(1)}, f32[768]{0:T(1024)}, u32[]{:S(2)}) copy-start(f32[768]{0:T(1024)} %reshape.489) | copy-start | bytes 9220
  165.8 6.8 %copy-start.29 = (f32[768]{0:T(1024)S(1)}, f32[768]{0:T(1024)}, u32[]{:S(2)}) copy-start(f32[768]{0:T(1024)} %reshape.490) | copy-start | bytes 9220
  165.8 6.8 %copy-start.37 = (f32[256]{0:T(256)S(1)}, f32[256]{0:T(256)}, u32[]{:S(2)}) copy-start(f32[256]{0:T(256)} %copy-done.36) | copy-start | bytes 3076
  165.8 6.8 %copy-start.42 = (f32[256]{0:T(256)S(1)}, f32[256]{0:T(256)}, u32[]{:S(2)}) copy-start(f32[256]{0:T(256)} %copy-done.41) | copy-start | bytes 3076
  172.6 3.8 %copy-start.7 = (f32[1,256,768]{2,1,0:T(8,128)S(1)}, f32[1,256,768]{2,1,0:T(8,128)}, u32[]{:S(2)}) copy-start(f32[1,256,768]{2,1,0:T(8,128)} %param.33) | copy-start | bytes 2359300
  172.6 3.8 %copy-start.11 = (bf16[256,3072]{1,0:T(8,128)(2,1)S(1)}, bf16[256,3072]{1,0:T(8,128)(2,1)}, u32[]{:S(2)}) copy-start(bf16[256,3072]{1,0:T(8,128)(2,1)} %copy-done.10) | copy-start | bytes 4718596
  280.3 4.4 %copy-start.25 = (f32[2,48,3072]{2,1,0:T(8,128)S(1)}, f32[2,48,3072]{2,1,0:T(8,128)}, u32[]{:S(2)}) copy-start(f32[2,48,3072]{2,1,0:T(8,128)} %get-tuple-element.31) | copy-start | bytes 3538948
  280.3 5.4 %copy-start.24 = (f32[2,192,768]{2,1,0:T(8,128)S(1)}, f32[2,192,768]{2,1,0:T(8,128)}, u32[]{:S(2)}) copy-start(f32[2,192,768]{2,1,0:T(8,128)} %get-tuple-element.32) | copy-start | bytes 3538948
  (1 other events, 1.0 us)

commit v3 on v2

--- a/solution.py
+++ b/solution.py
@@ -134,7 +134,17 @@
 def gather_kernel(count, streams, *refs):
     own = refs[:streams]
     whole = refs[streams : 2 * streams]
-    ring_send, ring_recv, pair_send, pair_recv, local_sem = refs[2 * streams :]
+    (
+        ring_send,
+        ring_recv,
+        pair_send,
+        pair_recv,
+        side_send,
+        side_recv,
+        late_send,
+        late_recv,
+        local_sem,
+    ) = refs[2 * streams :]
     me = lax.axis_index("shard")
     rep = lax.axis_index("rep")
     core = rep % 2
@@ -144,7 +154,31 @@
         {"shard": ring_index((place + count - 1) % count, count)},
     )
     partner = {"rep": rep + 1 - 2 * core}
-    greet((*ways, partner))
+    side = (rep // 2) % 2
+    across = {"rep": rep + 2 * (1 - 2 * side)}
+    greet((*ways, partner, across))
+
+    def columns(i):
+        width = own[i].shape[-1]
+        if width % 384:
+            return (pl.ds(0, width), None, None)
+        third = width // 3
+        mine = pl.ds(pl.multiple_of(side * third, 128), 2 * third)
+        give = pl.ds(pl.multiple_of(2 * side * third, 128), third)
+        take = pl.ds(pl.multiple_of(2 * (1 - side) * third, 128), third)
+        return (mine, give, take)
+
+    shares = [columns(i) for i in range(streams)]
+    sides = {}
+
+    def pass_on(i, way, step):
+        slot = way * ring_steps(i, count)[0] + step - 1
+        take = shares[i][2]
+        sides[(i, slot)].wait_recv()
+        landed = whole[i].at[owner_from(way, step), core, :, take]
+        late = remote(landed, landed, late_send.at[i, slot], late_recv.at[i, slot], partner)
+        late.start()
+        locals_.append(late)
 
     def owner_from(way, step):
         offset = count - step if way == 0 else step
@@ -164,16 +198,17 @@
                 if step > 0:
                     hops[(i, way)].wait_recv()
                     owner = owner_from(way, step)
-                    landed = whole[i].at[owner, core]
+                    landed = whole[i].at[owner, core, :, shares[i][0]]
                     cross = remote(
                         landed, landed, pair_send.at[i, slot - 1], pair_recv.at[i, slot - 1], partner
                     )
                 if step < steps[way]:
                     owner = owner_from(way, step)
-                    source = own[i].at[core] if step == 0 else whole[i].at[owner, core]
+                    into = whole[i].at[owner, core, :, shares[i][0]]
+                    source = own[i].at[core, :, shares[i][0]] if step == 0 else into
                     hop = remote(
                         source,
-                        whole[i].at[owner, core],
+                        into,
                         ring_send.at[i, slot],
                         ring_recv.at[i, slot],
                         ways[way],
@@ -182,8 +217,22 @@
                     hops[(i, way)] = hop
                     pending.append(hop)
                 if step > 0:
+                    if shares[i][1] is not None:
+                        given = whole[i].at[owner_from(way, step), core, :, shares[i][1]]
+                        aside = remote(
+                            given,
+                            given,
+                            side_send.at[i, slot - 1],
+                            side_recv.at[i, slot - 1],
+                            across,
+                        )
+                        aside.start()
+                        sides[(i, slot - 1)] = aside
+                        pending.append(aside)
                     cross.start()
                     locals_.append(cross)
+                if step > 1 and shares[i][1] is not None:
+                    pass_on(i, way, step - 1)
         if step == 0:
             keep = [
                 pltpu.make_async_copy(own[i], whole[i].at[me], local_sem.at[i])
@@ -191,6 +240,10 @@
             ]
             for copy in keep:
                 copy.start()
+    for i in range(streams):
+        for way in range(2):
+            if shares[i][1] is not None:
+                pass_on(i, way, ring_steps(i, count)[way])
     for cross in locals_:
         cross.wait()
     for hop in pending:
@@ -209,7 +262,7 @@
         out_shape=[jax.ShapeDtypeStruct((count, *half.shape), half.dtype) for half in halves],
         in_specs=[pl.BlockSpec(memory_space=pltpu.VMEM)] * streams,
         out_specs=[pl.BlockSpec(memory_space=pl.ANY)] * streams,
-        scratch_shapes=[dma((streams, count - 1))] * 4 + [dma((streams,))],
+        scratch_shapes=[dma((streams, count - 1))] * 8 + [dma((streams,))],
         compiler_params=pltpu.CompilerParams(collective_id=0, has_side_effects=True),
     )(*halves)
     return [out.reshape(-1, out.shape[-1]) for out in outs]

time: 288 us -> 269 us (0.934)
  Pallas kernels: 179 us -> 160 us
    pallas_call x1, Pallas kernels: 78.8 us -> 61 us  [gather_all(): pl.pallas_call(functools.partial(gather_kernel, count, streams), out_shap...]
where the time goes in v3:
time: 269 us; the launch traced here: 268 us
  Pallas kernels  160 us (59%)
  matrix products  44.8 us (17%)
  local copies, waits for them, and re-layouts  41.3 us (15%)
  other arithmetic  20.2 us (8%)
    pallas_call x1, Pallas kernels, reduce_all(): pl.pallas_call(functools.partial(reduce_kernel, count, peer_bits, streams...  99.3 us
    pallas_call x1, Pallas kernels, gather_all(): pl.pallas_call(functools.partial(gather_kernel, count, streams), out_shap...  61 us
    dot_general x6, matrix products, times_transposed(): lax.dot_general(left, right, (((1,), (1,)), ((), ())), preferred_element_...  15.2 us
    dot_general x6, matrix products, matmul(): return jnp.dot(left, right, preferred_element_type=jnp.float32)  11.8 us
    dot_general x6, matrix products, token_sum(): lax.dot_general(left, right, (((0,), (0,)), ((), ())), preferred_element_...  10.3 us
    reshape x9, local copies, waits for them, and re-layouts, on_device(): term.reshape(shards, -1)  9.42 us
    concatenate x1, local copies, waits for them, and re-layouts, on_device(): jnp.concatenate([term.astype(jnp.bfloat16) for term in (query_term, key_t...  6.78 us
    concatenate x1, local copies, waits for them, and re-layouts, on_device(): jnp.concatenate(vectors).reshape(2, -1)  6.11 us

profile of v3, /device:TPU:0, one launch (start us, length us, event | category | flops | bytes accessed | tf_op | source)
XLA Modules:
  0.0 268.0 jit_solution(14810254116752192470)
XLA Ops:
  0.7 1.3 reduce_sum.173
  2.0 1.4 multiply_reduce_fusion.7
  3.4 6.1 %concatenate.13 = bf16[1152]{0:T(1024)(128)(2,1)S(1)} concatenate(bf16[96]{0:T(256)(128)(2,1)} %param.18, bf16[96]{0:T(256)(128)(2,1)} %param.19, bf16[96]{0:T(256)(128)(2,1)} %param.21, bf16[96]{0:T(256)(128)(2,1)} %param.24, bf16[96]{0:T(256)(128)(2,1)} %param.26, bf16[96]{0:T(256)(128)(2,1)} %param.27, bf16[96]{0:T(256)(128)(2,1)} %param.28, bf16[96]{0:T(256)(128)(2,1)} %param.32, ...), dimensions={0} | concatenate | bytes 4608 | tf_op jit(solution)/shard_map/concatenate | solution.py:498
  10.2 1.2 reduce_sum.191
  12.1 2.0 pad_maximum_fusion.1
  14.0 61.0 %shard_map.296 = (bf16[8,2,48,3072]{3,2,1,0:T(8,128)(2,1)}, bf16[8,2,48,3072]{3,2,1,0:T(8,128)(2,1)}, bf16[8,2,192,768]{3,2,1,0:T(8,128)(2,1)}, bf16[8,2,1,576]{3,2,1,0:T(2,128)(2,1)}) custom-call(bf16[2,48,3072]{2,1,0:T(8,128)(2,1)} %bitcast.161, bf16[2,48,3072]{2,1,0:T(8,128)(2,1)} %bitcast.167, bf16[2,192,768]{2,1,0:T(8,128)(2,1)} %bitcast.168, ...), custom_call_target="tpu_custom_call" | custom-call | tf_op jit(solution)/shard_map/pallas_call | solution.py:260
  75.1 0.9 reduce.9
  80.2 1.7 fusion.10
  81.9 0.9 copy.51
  82.8 1.7 fusion.9
  84.6 1.7 convolution_convert_fusion.8
  86.4 0.9 copy.52
  87.3 0.9 copy.50
  88.2 1.8 multiply_reduce_fusion
  91.4 2.3 fusion.39
  94.1 1.9 multiply_convert_fusion.1
  96.6 3.0 %fusion.40 = (f32[3072]{0:T(1024)}, bf16[256,3072]{1,0:T(8,128)(2,1)S(1)}) fusion(f32[256,3072]{1,0:T(8,128)S(1)} %get-tuple-element.72, bf16[3072,768]{1,0:T(8,128)(2,1)S(1)} %bitcast.176, f32[1,256,768]{2,1,0:T(8,128)S(1)} %copy-done.6), kind=kOutput, calls=%fused_computation.110 | convolution fusion | flops 1216803840 | bytes 10235904 | tf_op jit(solution)/shard_map/dot_general | solution.py:42
  99.6 2.3 fusion.8
  101.9 3.1 %multiply_reduce_fusion.1 = (f32[768]{0:T(1024)}, f32[256]{0:T(256)}, f32[256]{0:T(256)}, f32[768]{0:T(1024)}, f32[256,768]{1,0:T(8,128)}) fusion(f32[256,768]{1,0:T(8,128)S(1)} %get-tuple-element.70, f32[256]{0:T(256)S(1)} %add_rsqrt_fusion, f32[256]{0:T(256)S(1)} %broadcast_multiply_fusion.4, f32[768]{0:T(1024)S(1)} %copy-done.26, ...), kind=kOutput, calls=%fused_computation.52 | convolution fusion | flops 1209726976 | bytes 7877632 | tf_op jit(solution)/shard_map/dot_general | solution.py:42
  105.0 1.3 reshape.471
  106.3 1.3 reshape.468
  108.3 3.4 %fusion.35 = (f32[768]{0:T(1024)}, f32[256,768]{1,0:T(8,128)}) fusion(f32[256]{0:T(256)S(1)} %get-tuple-element.79, f32[256]{0:T(256)} %copy-done.41, f32[256,768]{1,0:T(8,128)} %copy-done.3, f32[256]{0:T(256)} %copy-done.36, f32[256]{0:T(256)S(1)} %get-tuple-element.80, f32[256,768]{1,0:T(8,128)} %get-tuple-element.73, f32[768]{0:T(1024)} %reshape.489, ...), kind=kLoop, calls=%fused_computation.105 | loop fusion | flops 1768704 | bytes 3155968 | tf_op jit(solution)/shard_map/reduce_sum | solution.py:547
  111.7 1.4 reshape.467
  113.1 1.3 reshape.469
  114.4 2.8 %convolution_convert_fusion.6 = bf16[256,768]{1,0:T(8,128)(2,1)} fusion(bf16[768,3072]{1,0:T(8,128)(2,1)} %bitcast.144, f32[256,768]{1,0:T(8,128)} %get-tuple-element.42), kind=kOutput, calls=%fused_computation.36 | convolution fusion | flops 302383104 | bytes 2359296 | tf_op jit(solution)/shard_map/dot_general | solution.py:42
  117.2 1.9 copy.54
  119.1 2.0 copy.55
  121.2 1.4 multiply_reduce_fusion.4
  122.6 3.0 %fusion.37 = (f32[12,64]{1,0:T(8,128)}, bf16[1,256,12,64]{1,3,2,0:T(8,128)(2,1)}) fusion(bf16[256,12,64]{0,2,1:T(8,128)(2,1)} %bitcast.158, f32[12,256,256]{1,2,0:T(8,128)S(1)} %get-tuple-element.68, f32[12,256]{1,0:T(8,128)S(1)} %log_add_fusion), kind=kOutput, calls=%fused_computation.107 | convolution fusion | flops 103415040 | bytes 3947520 | tf_op jit(solution)/shard_map/chlm,clhd->cmhd/dot_general | solution.py:78
  125.7 0.9 multiply_convert_fusion
  129.1 1.8 fusion.16
  131.0 1.9 convolution_add_fusion.2
  132.9 2.7 %multiply_reduce_fusion.2 = (f32[768]{0:T(1024)}, f32[256]{0:T(256)}, f32[256]{0:T(256)}, f32[768]{0:T(1024)}, f32[256,768]{1,0:T(8,128)S(1)}) fusion(f32[1,256,768]{2,1,0:T(8,128)S(1)} %copy-done.2, f32[256]{0:T(256)S(1)} %copy-done.39, f32[256]{0:T(256)S(1)} %copy-done.35, f32[768]{0:T(1024)S(1)} %copy-done.31, f32[256,768]{1,0:T(8,128)S(1)} %convolution_add_fusion.2, ...), kind=kOutput, calls=%fused_computation.53 | convolution fusion | flops 303953920 | bytes 3945472 | tf_op jit(solution)/shard_map/dot_general | solution.py:42
  135.6 1.4 reshape.463
  138.3 1.9 add_bitcast_fusion
  140.7 0.7 reshape.464
  141.5 0.8 concatenate.15
  142.3 0.7 reshape_reshape.14.refs_3_
  143.0 1.5 convolution_convert_fusion.2
  145.4 2.5 pad_maximum_fusion
  148.0 6.8 %copy.60 = bf16[768,3072]{1,0:T(8,128)(2,1)} copy(bf16[768,3072]{0,1:T(8,128)(2,1)} %pad_maximum_fusion) | data formatting | bytes 9437184 | tf_op jit(solution)/shard_map/concatenate | solution.py:595
  154.8 3.7 %convolution_convert_fusion.1 = bf16[768,3072]{1,0:T(8,128)(2,1)} fusion(bf16[256,3072]{1,0:T(8,128)(2,1)S(1)} %copy-done.22, f32[256,768]{1,0:T(8,128)S(1)} %copy-done.4, f32[768]{0:T(1024)S(1)} %copy-done.29, f32[768]{0:T(1024)S(1)} %copy-done.27, f32[256]{0:T(256)S(1)} %copy-done.42, f32[256]{0:T(256)S(1)} %copy-done.37), kind=kOutput, calls=%fused_computation.1 | convolution fusion | flops 1211301888 | bytes 7086080 | tf_op jit(solution)/shard_map/dot_general | solution.py:48
  158.6 3.7 %fusion.41 = bf16[3072,768]{1,0:T(8,128)(2,1)} fusion(bf16[256,3072]{1,0:T(8,128)(2,1)S(1)} %copy-done.11, f32[1,256,768]{2,1,0:T(8,128)S(1)} %copy-done.7), kind=kOutput, calls=%fused_computation.111 | convolution fusion | flops 1207959552 | bytes 7077888 | tf_op jit(solution)/shard_map/dot_general | solution.py:48
  162.3 99.3 %shard_map.297 = (f32[2,48,3072]{2,1,0:T(8,128)}, f32[2,48,3072]{2,1,0:T(8,128)}, f32[2,192,768]{2,1,0:T(8,128)}, f32[2,1,576]{2,1,0:T(1,128)}) custom-call(bf16[8,2,48,3072]{3,2,1,0:T(8,128)(2,1)} %bitcast.137, bf16[8,2,48,3072]{3,2,1,0:T(8,128)(2,1)} %bitcast.136, bf16[8,2,192,768]{3,2,1,0:T(8,128)(2,1)} %bitcast.135, f32[8,2,1,576]{3,2,1,0:T(1,128)} %reshape_reshape.14.refs_3_), custom_call_target="tpu_custom_call" | custom-call | tf_op jit(solution)/shard_map/pallas_call | solution.py:419
  261.6 0.9 reduce.10
  262.5 2.3 fusion.36
  266.0 1.0 copy.68
  267.0 1.0 copy.69
  (137 shorter events, 15.0 us)
Async XLA Ops:
  0.7 79.1 %copy-start = (f32[1,256,768]{2,1,0:T(8,128)S(1)}, f32[1,256,768]{2,1,0:T(8,128)}, u32[]{:S(2)}) copy-start(f32[1,256,768]{2,1,0:T(8,128)} %param.17) | copy-start | bytes 2359300
  2.0 78.1 %copy-start.34 = (f32[256]{0:T(256)}, f32[256]{0:T(256)S(1)}, u32[]{:S(2)}) copy-start(f32[256]{0:T(256)S(1)} %broadcast_multiply_fusion.5) | copy-start | bytes 3076
  3.4 76.8 %copy-start.38 = (f32[256]{0:T(256)}, f32[256]{0:T(256)S(1)}, u32[]{:S(2)}) copy-start(f32[256]{0:T(256)S(1)} %add_rsqrt_fusion.1) | copy-start | bytes 3076
  78.2 6.4 %copy-start.30 = (f32[768]{0:T(1024)}, f32[768]{0:T(1024)S(1)}, u32[]{:S(2)}) copy-start(f32[768]{0:T(1024)S(1)} %reshape.484) | copy-start | bytes 9220
  88.2 2.4 copy-start.18
  90.0 1.4 copy-start.1
  90.0 1.4 copy-start.40
  90.0 4.0 %slice-start = ((s8[4718592]{0:T(1024)(128)(4,1)}), s8[4194304]{0:T(1024)(128)(4,1)S(1)}, s32[]{:S(2)}) async-start(s8[4718592]{0:T(1024)(128)(4,1)} %bitcast.170), calls=%async_computation | async-start | bytes 8388608
  90.6 3.4 %copy-start.26 = (f32[768]{0:T(1024)S(1)}, f32[768]{0:T(1024)}, u32[]{:S(2)}) copy-start(f32[768]{0:T(1024)} %reshape.489) | copy-start | bytes 9220
  90.6 3.4 %copy-start.28 = (f32[768]{0:T(1024)S(1)}, f32[768]{0:T(1024)}, u32[]{:S(2)}) copy-start(f32[768]{0:T(1024)} %reshape.490) | copy-start | bytes 9220
  90.6 3.4 %copy-start.43 = (f32[3072]{0:T(1024)S(1)}, f32[3072]{0:T(1024)}, u32[]{:S(2)}) copy-start(f32[3072]{0:T(1024)} %reshape.491) | copy-start | bytes 36868
  90.7 3.4 %slice-start.1 = ((s8[4718592]{0:T(1024)(128)(4,1)}), s8[524288]{0:T(1024)(128)(4,1)S(1)}, s32[]{:S(2)}) async-start(s8[4718592]{0:T(1024)(128)(4,1)} %bitcast.170), calls=%async_computation.1 | async-start | bytes 1048576
  91.3 2.6 copy-start.8
  93.7 8.2 %copy-start.3 = (f32[256,768]{1,0:T(8,128)}, f32[256,768]{1,0:T(8,128)S(1)}, u32[]{:S(2)}) copy-start(f32[256,768]{1,0:T(8,128)S(1)} %get-tuple-element.70) | copy-start | bytes 2359300
  93.7 8.2 %copy-start.36 = (f32[256]{0:T(256)}, f32[256]{0:T(256)S(1)}, u32[]{:S(2)}) copy-start(f32[256]{0:T(256)S(1)} %broadcast_multiply_fusion.4) | copy-start | bytes 3076
  93.7 2.5 slice-start.2
  94.1 7.9 %copy-start.41 = (f32[256]{0:T(256)}, f32[256]{0:T(256)S(1)}, u32[]{:S(2)}) copy-start(f32[256]{0:T(256)S(1)} %add_rsqrt_fusion) | copy-start | bytes 3076
  94.1 2.4 copy-start.6
  94.1 2.5 slice-start.3
  96.0 3.6 %copy-start.10 = (bf16[256,3072]{1,0:T(8,128)(2,1)}, bf16[256,3072]{1,0:T(8,128)(2,1)S(1)}, u32[]{:S(2)}) copy-start(bf16[256,3072]{1,0:T(8,128)(2,1)S(1)} %get-tuple-element.71) | copy-start | bytes 4718596
  96.6 3.0 %copy-start.44 = (f32[768]{0:T(1024)S(1)}, f32[768]{0:T(1024)}, u32[]{:S(2)}) copy-start(f32[768]{0:T(1024)} %reshape.492) | copy-start | bytes 9220
  99.6 2.3 copy-start.21
  121.2 4.5 %copy-start.19 = (bf16[256,768]{0,1:T(8,128)(2,1)S(1)}, bf16[256,768]{0,1:T(8,128)(2,1)}, u32[]{:S(2)}) copy-start(bf16[256,768]{0,1:T(8,128)(2,1)} %copy.50) | copy-start | bytes 1179652
  121.2 4.5 %copy-start.20 = (bf16[256,768]{0,1:T(8,128)(2,1)S(1)}, bf16[256,768]{0,1:T(8,128)(2,1)}, u32[]{:S(2)}) copy-start(bf16[256,768]{0,1:T(8,128)(2,1)} %copy.54) | copy-start | bytes 1179652
  125.7 1.6 copy-start.17
  126.6 1.8 copy-start.33
  127.3 3.7 %copy-start.12 = (bf16[12,64,256]{2,1,0:T(8,128)(2,1)}, bf16[12,64,256]{2,1,0:T(8,128)(2,1)S(1)}, u32[]{:S(2)}) copy-start(bf16[12,64,256]{2,1,0:T(8,128)(2,1)S(1)} %fusion.11) | copy-start | bytes 1179652
  127.8 1.4 copy-start.14
  127.8 5.1 %copy-start.2 = (f32[1,256,768]{2,1,0:T(8,128)S(1)}, f32[1,256,768]{2,1,0:T(8,128)}, u32[]{:S(2)}) copy-start(f32[1,256,768]{2,1,0:T(8,128)} %param.17) | copy-start | bytes 2359300
  127.8 5.1 %copy-start.23 = (bf16[1,256,12,64]{1,3,2,0:T(8,128)(2,1)S(1)}, bf16[1,256,12,64]{1,3,2,0:T(8,128)(2,1)}, u32[]{:S(2)}) copy-start(bf16[1,256,12,64]{1,3,2,0:T(8,128)(2,1)} %get-tuple-element.48) | copy-start | bytes 1179652
  127.8 5.1 %copy-start.31 = (f32[768]{0:T(1024)S(1)}, f32[768]{0:T(1024)}, u32[]{:S(2)}) copy-start(f32[768]{0:T(1024)} %copy-done.30) | copy-start | bytes 9220
  127.8 5.1 %copy-start.35 = (f32[256]{0:T(256)S(1)}, f32[256]{0:T(256)}, u32[]{:S(2)}) copy-start(f32[256]{0:T(256)} %copy-done.34) | copy-start | bytes 3076
  127.8 5.1 %copy-start.39 = (f32[256]{0:T(256)S(1)}, f32[256]{0:T(256)}, u32[]{:S(2)}) copy-start(f32[256]{0:T(256)} %copy-done.38) | copy-start | bytes 3076
  130.9 7.4 %copy-start.5 = (f32[256,768]{1,0:T(8,128)S(1)}, f32[256,768]{1,0:T(8,128)}, u32[]{:S(2)}) copy-start(f32[256,768]{1,0:T(8,128)} %get-tuple-element.42) | copy-start | bytes 2359300
  132.9 7.3 %copy-start.9 = (bf16[12,64,256]{2,1,0:T(8,128)(2,1)S(1)}, bf16[12,64,256]{2,1,0:T(8,128)(2,1)}, u32[]{:S(2)}) copy-start(bf16[12,64,256]{2,1,0:T(8,128)(2,1)} %copy-done.8) | copy-start | bytes 1179652
  135.6 5.9 %copy-start.32 = (f32[8,384]{1,0:T(8,128)S(1)}, f32[8,384]{1,0:T(8,128)}, u32[]{:S(2)}) copy-start(f32[8,384]{1,0:T(8,128)} %reshape.471) | copy-start | bytes 36868
  140.2 4.3 %copy-start.13 = (bf16[12,64,256]{2,1,0:T(8,128)(2,1)S(1)}, bf16[12,64,256]{2,1,0:T(8,128)(2,1)}, u32[]{:S(2)}) copy-start(bf16[12,64,256]{2,1,0:T(8,128)(2,1)} %copy-done.12) | copy-start | bytes 1179652
  140.2 4.7 %copy-start.15 = (bf16[1,256,12,64]{1,3,2,0:T(8,128)(2,1)S(1)}, bf16[1,256,12,64]{1,3,2,0:T(8,128)(2,1)}, u32[]{:S(2)}) copy-start(bf16[1,256,12,64]{1,3,2,0:T(8,128)(2,1)} %copy-done.14) | copy-start | bytes 1179652
  148.0 6.8 %copy-start.4 = (f32[256,768]{1,0:T(8,128)S(1)}, f32[256,768]{1,0:T(8,128)}, u32[]{:S(2)}) copy-start(f32[256,768]{1,0:T(8,128)} %copy-done.3) | copy-start | bytes 2359300
  148.0 6.8 %copy-start.22 = (bf16[256,3072]{1,0:T(8,128)(2,1)S(1)}, bf16[256,3072]{1,0:T(8,128)(2,1)}, u32[]{:S(2)}) copy-start(bf16[256,3072]{1,0:T(8,128)(2,1)} %copy-done.21) | copy-start | bytes 4718596
  148.0 6.8 %copy-start.27 = (f32[768]{0:T(1024)S(1)}, f32[768]{0:T(1024)}, u32[]{:S(2)}) copy-start(f32[768]{0:T(1024)} %reshape.489) | copy-start | bytes 9220
  148.0 6.8 %copy-start.29 = (f32[768]{0:T(1024)S(1)}, f32[768]{0:T(1024)}, u32[]{:S(2)}) copy-start(f32[768]{0:T(1024)} %reshape.490) | copy-start | bytes 9220
  148.0 6.8 %copy-start.37 = (f32[256]{0:T(256)S(1)}, f32[256]{0:T(256)}, u32[]{:S(2)}) copy-start(f32[256]{0:T(256)} %copy-done.36) | copy-start | bytes 3076
  148.0 6.8 %copy-start.42 = (f32[256]{0:T(256)S(1)}, f32[256]{0:T(256)}, u32[]{:S(2)}) copy-start(f32[256]{0:T(256)} %copy-done.41) | copy-start | bytes 3076
  154.8 3.8 %copy-start.7 = (f32[1,256,768]{2,1,0:T(8,128)S(1)}, f32[1,256,768]{2,1,0:T(8,128)}, u32[]{:S(2)}) copy-start(f32[1,256,768]{2,1,0:T(8,128)} %param.33) | copy-start | bytes 2359300
  154.8 3.8 %copy-start.11 = (bf16[256,3072]{1,0:T(8,128)(2,1)S(1)}, bf16[256,3072]{1,0:T(8,128)(2,1)}, u32[]{:S(2)}) copy-start(bf16[256,3072]{1,0:T(8,128)(2,1)} %copy-done.10) | copy-start | bytes 4718596
  261.6 4.4 %copy-start.25 = (f32[2,48,3072]{2,1,0:T(8,128)S(1)}, f32[2,48,3072]{2,1,0:T(8,128)}, u32[]{:S(2)}) copy-start(f32[2,48,3072]{2,1,0:T(8,128)} %get-tuple-element.31) | copy-start | bytes 3538948
  261.6 5.4 %copy-start.24 = (f32[2,192,768]{2,1,0:T(8,128)S(1)}, f32[2,192,768]{2,1,0:T(8,128)}, u32[]{:S(2)}) copy-start(f32[2,192,768]{2,1,0:T(8,128)} %get-tuple-element.32) | copy-start | bytes 3538948
  (1 other events, 1.0 us)
